TPU v7x, 32 devices: a whole 2x2x4 slice. The times are simulated.
32 devices in a mesh: tgt: 4 (over y, x), sup: 8 (over z, core).
Axes of the slice: x: 2, y: 2, z: 4, core: 2. Of those that a mesh axis runs over, the one named last changes fastest.
Arguments:
- support: float32 [32, 3, 1024], P(('sup', 'tgt')), may hold values from -14 to 14
- coeffs: float32 [32, 100], P('sup'), may hold values from -10 to 10
- targets: float32 [32, 3, 1024], P(('tgt', 'sup')), may hold values from -14 to 14
- labels: float32 [32, 100], P(('tgt', 'sup')), may hold values from -5 to 5
Outputs:
- support_grad: float32 [32, 3, 1024], P(('sup', 'tgt'))
- residual: float32 [32, 100], P(('tgt', 'sup'))
All inputs are finite; a program needn't handle non-finite values.
Results may differ from a plain program's by a relative error of at most 0.000064.
Values sent between devices are 32-bit elements; how exact they have to be, the bound alone decides.
No kernel may reach another device: no remote copies, remote signals or barrier semaphores. Data moves between devices by JAX's collectives and lax.ppermute only.
A program may use at most 128 MiB of HBM per device.

v0:
```python
import math

import jax
import jax.numpy as jnp
from jax import lax
from jax.sharding import PartitionSpec as P

SIDE = 32
DEPTH = 3


WEIGHT_VAR = 1.6
BIAS_VAR = 0.1


def spread(values):
    side_cells = values.shape[0]
    padded = jnp.pad(values, ((1, 1), (1, 1), (0, 0)))
    summed = jnp.zeros_like(values)
    for row_shift in range(3):
        for col_shift in range(3):
            summed = (
                summed
                + padded[row_shift : row_shift + side_cells, col_shift : col_shift + side_cells]
            )
    return summed / 9.0


def self_levels(images):
    image_count = images.shape[0]
    energy = jnp.mean(images * images, axis=1)
    kernel_level = WEIGHT_VAR * spread(energy.T.reshape(SIDE, SIDE, image_count)) + BIAS_VAR
    levels = [kernel_level]
    for layer_idx in range(DEPTH - 1):
        activated = 2.0 / math.pi * jnp.arcsin(2.0 * kernel_level / (1.0 + 2.0 * kernel_level))
        kernel_level = WEIGHT_VAR * spread(activated) + BIAS_VAR
        levels.append(kernel_level)
    return levels


def pair_kernel(support, targets):
    sup_count = support.shape[0]
    tgt_count = targets.shape[0]
    sup_levels = self_levels(support)
    tgt_levels = self_levels(targets)
    products = (
        jnp.einsum("scp,tcp->pst", support, targets, precision=lax.Precision.HIGHEST)
        / support.shape[1]
    )
    kernel_level = (
        WEIGHT_VAR * spread(products.reshape(SIDE, SIDE, sup_count * tgt_count)) + BIAS_VAR
    )
    activated = kernel_level
    for layer_idx in range(DEPTH):
        sup_gain = lax.rsqrt(1.0 + 2.0 * sup_levels[layer_idx])
        tgt_gain = lax.rsqrt(1.0 + 2.0 * tgt_levels[layer_idx])
        correlation = (
            2.0
            * kernel_level.reshape(SIDE, SIDE, sup_count, tgt_count)
            * sup_gain[:, :, :, None]
            * tgt_gain[:, :, None, :]
        )
        activated = 2.0 / math.pi * jnp.arcsin(correlation)
        if layer_idx + 1 < DEPTH:
            kernel_level = (
                WEIGHT_VAR * spread(activated.reshape(SIDE, SIDE, sup_count * tgt_count)) + BIAS_VAR
            )
    return WEIGHT_VAR * jnp.mean(activated, axis=(0, 1)) + BIAS_VAR


def product(left, right):
    return jnp.dot(left, right, precision=lax.Precision.HIGHEST, preferred_element_type=jnp.float32)


def local(support, coeffs, targets, labels):
    tgt_dev = targets.shape[0]
    block = lax.all_gather(support, "tgt", axis=0, tiled=True)
    group, group_labels = (
        lax.all_gather(targets, "sup", axis=0, tiled=True),
        lax.all_gather(labels, "sup", axis=0, tiled=True),
    )
    theta, pullback = jax.vjp(lambda images: pair_kernel(images, group), block)
    predicted = lax.psum(product(theta.T, coeffs), "sup")
    misfit = predicted - group_labels
    residual = lax.dynamic_slice_in_dim(misfit, lax.axis_index("sup") * tgt_dev, tgt_dev, 0)
    block_grad = pullback(product(coeffs, misfit.T))[0]
    support_grad = lax.psum_scatter(block_grad, "tgt", scatter_dimension=0, tiled=True)
    return (support_grad, residual)


def solution(mesh):
    return jax.shard_map(
        local,
        mesh=mesh,
        in_specs=(
            P(("sup", "tgt"), None, None),
            P("sup", None),
            P(("tgt", "sup"), None, None),
            P(("tgt", "sup"), None),
        ),
        out_specs=(P(("sup", "tgt"), None, None), P(("tgt", "sup"), None)),
        check_vma=False,
    )
```

profile of v0, /device:TPU:0, one launch (start us, length us, event | category | flops | bytes accessed | tf_op | source)
XLA Modules:
  0.0 127.9 jit_solution(11291109133535098446)
XLA Ops:
  0.7 0.7 copy.146
  1.4 9.7 %all_gather.9 = f32[4,3,1024]{2,1,0:T(4,128)S(1)} all-gather(f32[1,3,1024]{2,1,0:T(4,128)S(1)} %copy.146), channel_id=1, replica_groups=mesh['tgt'=4,'sup'=8] {'tgt'}, dimensions={0}, use_global_device_ids=true | all-gather | bytes 61440 | tf_op jit(solution)/shard_map/all_gather | solution.py:77
  11.1 0.2 copy.196
  11.4 0.3 copy.194
  11.7 0.2 broadcast_multiply_fusion.4
  12.0 14.3 %all_gather.10 = f32[8,3,1024]{2,1,0:T(4,128)S(1)} all-gather(f32[1,3,1024]{2,1,0:T(4,128)S(1)} %copy.147), channel_id=1, replica_groups=mesh['tgt'=4,'sup'=8] {'sup'}, dimensions={0}, use_global_device_ids=true | all-gather | bytes 110592 | tf_op jit(solution)/shard_map/all_gather | solution.py:79
  26.3 0.2 copy.197
  26.6 0.2 copy.195
  26.8 0.9 add_rsqrt_fusion.1
  27.8 0.1 broadcast_bitcast_fusion.7
  27.9 2.7 %copy.149 = f32[8,3,1024]{1,0,2:T(8,128)} copy(f32[8,3,1024]{2,1,0:T(4,128)S(1)} %all_gather.10) | data formatting | bytes 196608 | tf_op jit(solution)/shard_map/all_gather | solution.py:79
  30.6 1.8 %copy.148 = f32[4,3,1024]{1,0,2:T(4,128)} copy(f32[4,3,1024]{2,1,0:T(4,128)S(1)} %all_gather.9) | data formatting | bytes 98304 | tf_op jit(solution)/shard_map/all_gather | solution.py:77
  32.4 9.7 %convolution_multiply_fusion = f32[1024,4,8]{2,1,0:T(4,128)S(1)} fusion(f32[4,3,1024]{1,0,2:T(4,128)} %copy.148, f32[8,3,1024]{1,0,2:T(8,128)} %copy.149), kind=kOutput, calls=%fused_computation | convolution fusion | flops 1212416 | bytes 278528 | tf_op jit(solution)/shard_map/jvp(scp,tcp->pst)/dot_general | solution.py:47
  42.1 0.9 copy.150
  43.0 0.2 reshape.78
  43.2 2.7 %add_multiply_fusion.3 = (f32[32,32,32]{1,0,2:T(8,128)S(1)}, f32[32,32,32]{1,0,2:T(8,128)S(1)}) fusion(f32[32,32,32]{1,2,0:T(8,128)S(1)} %get-tuple-element.40, f32[32,32,32]{1,2,0:T(8,128)S(1)} %get-tuple-element.41, f32[32,32,32]{1,0,2:T(8,128)S(1)} %reshape.78), kind=kLoop, calls=%fused_computation.116 | loop fusion | flops 589824 | bytes 655360 | tf_op jit(solution)/shard_map/jvp()/mul | solution.py:63
  45.9 0.7 add_multiply_fusion.11
  46.6 0.2 broadcast_multiply_fusion.3
  46.9 0.3 add_multiply_fusion.6
  47.2 0.3 add_rsqrt_fusion
  47.5 0.1 copy.165
  47.6 0.1 broadcast_bitcast_fusion.5
  47.7 3.3 %add_multiply_fusion.1 = (f32[32,32,32]{1,0,2:T(8,128)S(1)}, f32[32,32,32]{1,0,2:T(8,128)}) fusion(f32[32,32,32]{1,2,0:T(8,128)S(1)} %get-tuple-element.42, f32[32,32,32]{1,2,0:T(8,128)S(1)} %get-tuple-element.43, f32[32,32,32]{1,0,2:T(8,128)S(1)} %get-tuple-element.26), kind=kLoop, calls=%fused_computation.114 | loop fusion | flops 589824 | bytes 655360 | tf_op jit(solution)/shard_map/jvp()/mul | solution.py:63
  51.0 0.7 add_multiply_fusion.9
  51.7 0.8 broadcast_multiply_fusion.2
  52.6 0.3 add_multiply_fusion.5
  52.9 0.3 fusion.85
  53.2 0.1 copy.169
  53.3 0.1 broadcast_bitcast_fusion.3
  53.4 2.3 %multiply_reduce_fusion = (f32[32]{0:T(128)S(1)}, f32[32,32,32]{1,0,2:T(8,128)S(1)}) fusion(f32[32,32,32]{1,2,0:T(8,128)S(1)} %get-tuple-element.44, f32[32,32,32]{1,2,0:T(8,128)S(1)} %get-tuple-element.45, f32[32,32,32]{1,0,2:T(8,128)S(1)} %get-tuple-element.22), kind=kLoop, calls=%fused_computation.112 | loop fusion | flops 622560 | bytes 524416 | tf_op jit(solution)/shard_map/jvp()/reduce_sum | solution.py:68
  55.7 0.1 add.505
  55.7 0.2 fusion.155
  55.9 16.9 %psum.7 = f32[8,100]{1,0:T(8,128)S(1)} all-reduce(f32[8,100]{1,0:T(8,128)S(1)} %fusion.155), channel_id=1, replica_groups=mesh['tgt'=4,'sup'=8] {'sup'}, use_global_device_ids=true, to_apply=%region_3.4 | all-reduce | flops 800 | bytes 6400 | tf_op jit(solution)/shard_map/psum | solution.py:83
  72.8 8.6 %all-gather = f32[8,1,100]{2,1,0:T(1,128)S(1)} all-gather(f32[1,1,100]{2,1,0:T(1,128)S(1)} %bitcast.95), channel_id=1, replica_groups=mesh['tgt'=4,'sup'=8] {'sup'}, dimensions={0}, use_global_device_ids=true | all-gather | bytes 3600 | tf_op jit(solution)/shard_map/all_gather | solution.py:80
  81.4 0.1 fusion
  81.6 1.4 %fusion.35 = f32[32,32,4]{1,2,0:T(4,128)S(1)} fusion(f32[32,32,32]{1,0,2:T(8,128)S(1)} %get-tuple-element.19, f32[4,8]{1,0:T(4,128)S(1)} %fusion, f32[32,32,8]{1,2,0:T(8,128)S(1)} %copy.169, f32[32,32,4]{1,2,0:T(4,128)} %copy-done.16), kind=kLoop, calls=%fused_computation.84 | loop fusion | flops 323584 | bytes 196736 | tf_op jit(solution)/shard_map/transpose(jvp())/reduce_sum | solution.py:58
  83.0 0.9 fusion.144
  83.9 0.9 broadcast_bitcast_fusion.2
  84.8 0.1 broadcast_in_dim.16
  84.8 2.3 %fusion.47 = f32[32,32,32]{1,0,2:T(8,128)S(1)} fusion(f32[32,32,32]{1,2,0:T(8,128)} %broadcast_bitcast_fusion.2, f32[32,32,32]{1,2,0:T(8,128)S(1)} %get-tuple-element.44, f32[32]{0:T(128)S(1)} %broadcast_in_dim.16, f32[32,32,32]{1,0,2:T(8,128)S(1)} %get-tuple-element.19, f32[32,32,32]{1,2,0:T(8,128)S(1)} %get-tuple-element.45), kind=kLoop, calls=%fused_computation.105 | loop fusion | flops 294912 | bytes 655488 | tf_op jit(solution)/shard_map/transpose(jvp())/div | solution.py:26
  87.1 0.4 pad_add_fusion.2
  87.7 1.4 %fusion.46 = (f32[32,32,32]{1,0,2:T(8,128)S(1)}, f32[32,32,32]{1,0,2:T(8,128)S(1)}) fusion(f32[32,32,32]{1,2,0:T(8,128)S(1)} %broadcast_bitcast_fusion.1, f32[32,32,32]{1,2,0:T(8,128)S(1)} %copy-done.3, f32[32,32,32]{1,0,2:T(8,128)S(1)} %copy-done.1, f32[32,32,32]{1,2,0:T(8,128)S(1)} %copy-done.5, f32[32,32,32]{1,0,2:T(8,128)S(1)} %fusion.47, ...), kind=kLoop, calls=%fused_computation.103 | loop fusion | flops 524288 | bytes 1048576 | tf_op jit(solution)/shard_map/transpose(jvp())/div | solution.py:26
  89.1 0.4 pad_add_fusion.1
  89.7 1.5 %fusion.45 = (f32[32,32,32]{1,0,2:T(8,128)S(1)}, f32[32,32,32]{1,0,2:T(8,128)S(1)}) fusion(f32[32,32,32]{1,2,0:T(8,128)S(1)} %broadcast_bitcast_fusion, f32[32,32,32]{1,2,0:T(8,128)S(1)} %get-tuple-element.40, f32[32,32,32]{1,0,2:T(8,128)S(1)} %get-tuple-element.27, f32[32,32,32]{1,2,0:T(8,128)S(1)} %get-tuple-element.41, ...), kind=kLoop, calls=%fused_computation.101 | loop fusion | flops 524288 | bytes 1048576 | tf_op jit(solution)/shard_map/transpose(jvp())/div | solution.py:26
  91.2 0.8 fusion.43
  92.1 0.8 fusion.39
  92.9 0.1 pad_add_fusion.23
  93.0 0.2 fusion.100
  93.2 0.1 pad_add_fusion.22
  93.3 0.2 fusion.91
  93.5 0.1 pad_add_fusion.21
  93.6 0.2 fusion.139
  93.8 0.1 div.122
  93.8 0.4 pad_add_fusion
  94.3 0.8 fusion.31
  95.0 0.2 div.109
  95.3 1.1 copy.180
  96.4 11.1 %fusion.156 = f32[1024,4,3]{1,2,0:T(4,128)} fusion(f32[1024,4,8]{2,1,0:T(4,128)S(1)} %copy.180, f32[8,3,1024]{1,0,2:T(8,128)} %copy.149), kind=kOutput, calls=%fused_computation.323 | convolution fusion | flops 1179648 | bytes 278528 | tf_op jit(solution)/shard_map/transpose(jvp(scp,tcp->pst))/dot_general | solution.py:47
  107.5 1.8 %copy.182 = f32[1024,4,3]{0,1,2:T(4,128)S(1)} copy(f32[1024,4,3]{1,2,0:T(4,128)} %fusion.156) | data formatting | bytes 98304 | tf_op jit(solution)/shard_map/transpose(jvp(scp,tcp->pst))/dot_general | solution.py:47
  109.5 16.1 %all-reduce.63 = f32[4,3,1024]{2,1,0:T(4,128)S(1)} all-reduce(f32[4,3,1024]{2,1,0:T(4,128)S(1)} %copy.192), channel_id=2, replica_groups=mesh['tgt'=4,'sup'=8] {'tgt'}, use_global_device_ids=true, to_apply=%region_7.8.clone | all-reduce | flops 12288 | bytes 98304
  125.5 0.6 dynamic-slice
  126.1 0.7 constant_dynamic-slice_fusion
  126.8 0.6 copy.193
  127.4 0.5 constant_dynamic-slice_fusion.1
  (64 shorter events, 0.9 us)
Async XLA Ops:
  0.6 55.1 %copy-start = (f32[4,100]{1,0:T(4,128)S(1)}, f32[4,100]{1,0:T(4,128)}, u32[]{:S(2)}) copy-start(f32[4,100]{1,0:T(4,128)} %param.5) | copy-start | bytes 4804
  0.6 11.3 %copy-start.20 = (f32[1,3,1024]{2,0,1:T(1,128)S(1)}, f32[1,3,1024]{2,0,1:T(1,128)}, u32[]{:S(2)}) copy-start(f32[1,3,1024]{2,0,1:T(1,128)} %param.6) | copy-start | bytes 36868
  11.1 19.5 %copy-start.6 = (f32[4,3,1024]{2,1,0:T(4,128)}, f32[4,3,1024]{2,1,0:T(4,128)S(1)}, u32[]{:S(2)}) copy-start(f32[4,3,1024]{2,1,0:T(4,128)S(1)} %all_gather.9) | copy-start | bytes 147460
  11.9 34.0 %copy-start.8 = (f32[32,32,4]{1,0,2:T(8,128)}, f32[32,32,4]{1,0,2:T(8,128)S(1)}, u32[]{:S(2)}) copy-start(f32[32,32,4]{1,0,2:T(8,128)S(1)} %get-tuple-element.29) | copy-start | bytes 49156
  12.0 15.9 %copy-start.12 = (f32[32,32,4]{1,2,0:T(4,128)}, f32[32,32,4]{1,2,0:T(4,128)S(1)}, u32[]{:S(2)}) copy-start(f32[32,32,4]{1,2,0:T(4,128)S(1)} %copy.155) | copy-start | bytes 49156
  43.0 3.9 %copy-start.17 = (f32[32,32,8]{1,0,2:T(8,128)S(1)}, f32[32,32,8]{1,0,2:T(8,128)}, u32[]{:S(2)}) copy-start(f32[32,32,8]{1,0,2:T(8,128)} %get-tuple-element.31) | copy-start | bytes 98308
  46.8 4.2 %copy-start.10 = (f32[32,32,4]{1,0,2:T(8,128)}, f32[32,32,4]{1,0,2:T(8,128)S(1)}, u32[]{:S(2)}) copy-start(f32[32,32,4]{1,0,2:T(8,128)S(1)} %get-tuple-element.25) | copy-start | bytes 49156
  46.9 4.1 %copy-start.14 = (f32[32,32,4]{1,2,0:T(4,128)}, f32[32,32,4]{1,2,0:T(4,128)S(1)}, u32[]{:S(2)}) copy-start(f32[32,32,4]{1,2,0:T(4,128)S(1)} %copy.163) | copy-start | bytes 49156
  47.7 5.7 %copy-start.2 = (f32[32,32,32]{1,2,0:T(8,128)}, f32[32,32,32]{1,2,0:T(8,128)S(1)}, u32[]{:S(2)}) copy-start(f32[32,32,32]{1,2,0:T(8,128)S(1)} %get-tuple-element.42) | copy-start | bytes 393220
  47.7 5.7 %copy-start.4 = (f32[32,32,32]{1,2,0:T(8,128)}, f32[32,32,32]{1,2,0:T(8,128)S(1)}, u32[]{:S(2)}) copy-start(f32[32,32,32]{1,2,0:T(8,128)S(1)} %get-tuple-element.43) | copy-start | bytes 393220
  52.6 3.1 %copy-start.16 = (f32[32,32,4]{1,2,0:T(4,128)}, f32[32,32,4]{1,2,0:T(4,128)S(1)}, u32[]{:S(2)}) copy-start(f32[32,32,4]{1,2,0:T(4,128)S(1)} %copy.167) | copy-start | bytes 49156
  52.6 20.2 %copy-start.21 = (f32[1,100]{1,0:T(1,128)S(1)}, f32[1,100]{1,0:T(1,128)}, u32[]{:S(2)}) copy-start(f32[1,100]{1,0:T(1,128)} %param.7) | copy-start | bytes 1204
  83.9 3.6 %copy-start.19 = (f32[32,32,4]{1,0,2:T(8,128)S(1)}, f32[32,32,4]{1,0,2:T(8,128)}, u32[]{:S(2)}) copy-start(f32[32,32,4]{1,0,2:T(8,128)} %get-tuple-element.37) | copy-start | bytes 49156
  84.8 2.8 %copy-start.1 = (f32[32,32,32]{1,0,2:T(8,128)S(1)}, f32[32,32,32]{1,0,2:T(8,128)}, u32[]{:S(2)}) copy-start(f32[32,32,32]{1,0,2:T(8,128)} %get-tuple-element.23) | copy-start | bytes 393220
  84.8 2.8 %copy-start.3 = (f32[32,32,32]{1,2,0:T(8,128)S(1)}, f32[32,32,32]{1,2,0:T(8,128)}, u32[]{:S(2)}) copy-start(f32[32,32,32]{1,2,0:T(8,128)} %copy-done.2) | copy-start | bytes 393220
  84.8 2.8 %copy-start.5 = (f32[32,32,32]{1,2,0:T(8,128)S(1)}, f32[32,32,32]{1,2,0:T(8,128)}, u32[]{:S(2)}) copy-start(f32[32,32,32]{1,2,0:T(8,128)} %copy-done.4) | copy-start | bytes 393220
  87.7 1.9 %copy-start.18 = (f32[32,32,4]{1,0,2:T(8,128)S(1)}, f32[32,32,4]{1,0,2:T(8,128)}, u32[]{:S(2)}) copy-start(f32[32,32,4]{1,0,2:T(8,128)} %get-tuple-element.39) | copy-start | bytes 49156
  89.7 1.6 %copy-start.13 = (f32[32,32,4]{1,2,0:T(4,128)S(1)}, f32[32,32,4]{1,2,0:T(4,128)}, u32[]{:S(2)}) copy-start(f32[32,32,4]{1,2,0:T(4,128)} %copy-done.12) | copy-start | bytes 49156
  89.7 2.4 %copy-start.15 = (f32[32,32,4]{1,2,0:T(4,128)S(1)}, f32[32,32,4]{1,2,0:T(4,128)}, u32[]{:S(2)}) copy-start(f32[32,32,4]{1,2,0:T(4,128)} %copy-done.14) | copy-start | bytes 49156
  91.2 1.8 %copy-start.11 = (f32[32,32,4]{1,0,2:T(8,128)S(1)}, f32[32,32,4]{1,0,2:T(8,128)}, u32[]{:S(2)}) copy-start(f32[32,32,4]{1,0,2:T(8,128)} %copy-done.10) | copy-start | bytes 49156
  91.2 2.1 %copy-start.9 = (f32[32,32,4]{1,0,2:T(8,128)S(1)}, f32[32,32,4]{1,0,2:T(8,128)}, u32[]{:S(2)}) copy-start(f32[32,32,4]{1,0,2:T(8,128)} %copy-done.8) | copy-start | bytes 49156
  107.5 1.8 %copy-start.7 = (f32[4,3,1024]{2,1,0:T(4,128)S(1)}, f32[4,3,1024]{2,1,0:T(4,128)}, u32[]{:S(2)}) copy-start(f32[4,3,1024]{2,1,0:T(4,128)} %copy-done.6) | copy-start | bytes 147460
  107.5 18.0 %copy-start.22 = (u32[32]{0:T(128)S(1)}, u32[32]{0:T(128)}, u32[]{:S(2)}) copy-start(u32[32]{0:T(128)} %constant.232) | copy-start | bytes 388
where the time goes:
time: 128 us
  blocking collectives  65.5 us (51%)
  other arithmetic  25.1 us (20%)
  matrix products  21.2 us (17%)
  local copies, waits for them, and re-layouts  14.8 us (12%)
    dot_general x2, matrix products, pair_kernel(): jnp.einsum('scp,tcp->pst', support, targets, precision=lax.Precision.HIGH...  20.9 us
    psum x1, blocking collectives, local(): predicted = lax.psum(product(theta.T, coeffs), 'sup')  16.9 us
    unnamed x1, blocking collectives  16.1 us
    all_gather x1, blocking collectives, local(): lax.all_gather(targets, 'sup', axis=0, tiled=True)  14.3 us
    all_gather x1, blocking collectives, local(): block = lax.all_gather(support, 'tgt', axis=0, tiled=True)  9.71 us
    all_gather x1, blocking collectives, local(): lax.all_gather(labels, 'sup', axis=0, tiled=True)  8.65 us
    div x6, other arithmetic, spread(): return summed / 9.0  6.42 us
    mul x2, other arithmetic, pair_kernel(): activated = 2.0 / math.pi * jnp.arcsin(correlation)  6 us

commit v1 on v0

v1 whole, which is shorter than its diff:
```python
import functools
import math

import jax
import jax.numpy as jnp
from jax import lax
from jax.experimental import pallas as pl
from jax.experimental.pallas import tpu as pltpu
from jax.sharding import Mesh
from jax.sharding import PartitionSpec as P

WEIGHT_VAR = 1.6
BIAS_VAR = 0.1
CH = 3
SUB = 8
LANE = 128
TWO_PI = 2.0 / math.pi
CHUNK = 8


def arcsine(x):
    a = jnp.abs(x)
    large = a > 0.5
    z = jnp.where(large, 0.5 - 0.5 * a, a * a)
    y = jnp.where(large, jnp.sqrt(z), a)
    p = 4.2163199048e-2 * z + 2.4181311049e-2
    p = p * z + 4.5470025998e-2
    p = p * z + 7.4953002686e-2
    p = p * z + 1.6666752422e-1
    y = p * z * y + y
    y = jnp.where(large, (0.5 * math.pi) - 2.0 * y, y)
    return jnp.where(x < 0.0, -y, y)


def box_sum(side):
    lane = lax.broadcasted_iota(jnp.int32, (SUB, LANE), 1)
    sub = lax.broadcasted_iota(jnp.int32, (SUB, LANE), 0)
    column = lane % side
    not_left, not_right = column != 0, column != side - 1
    inner_up, inner_down = lane >= side, lane < LANE - side
    not_top, not_bottom = sub != 0, sub != SUB - 1

    def apply(x):
        lanes, subs = x.ndim - 1, x.ndim - 2
        h = (
            x
            + jnp.where(not_left, pltpu.roll(x, 1, lanes), 0.0)
            + jnp.where(not_right, pltpu.roll(x, LANE - 1, lanes), 0.0)
        )
        above = pltpu.roll(h, side, lanes)
        below = pltpu.roll(h, LANE - side, lanes)
        above = jnp.where(
            inner_up, above, jnp.where(not_top, pltpu.roll(above, 1, subs), 0.0)
        )
        below = jnp.where(
            inner_down, below, jnp.where(not_bottom, pltpu.roll(below, SUB - 1, subs), 0.0)
        )
        return h + above + below

    return apply


def self_levels(images, box):
    energy = sum(image * image for image in images)
    level = (WEIGHT_VAR / (9 * CH)) * box(energy) + BIAS_VAR
    levels, gains = [], []
    for layer in range(3):
        gain = lax.rsqrt(1.0 + 2.0 * level)
        levels.append(level)
        gains.append(gain)
        if layer < 2:
            level = (WEIGHT_VAR * TWO_PI / 9) * box(
                arcsine(2.0 * level / (1.0 + 2.0 * level))
            ) + BIAS_VAR
    return levels, gains


def channels(ref, *lead):
    return [ref[lead + (slice(c * SUB, (c + 1) * SUB), slice(None))] for c in range(CH)]


def pair_body(side, pixels, row_of, own_ref, oth_ref, sup_ref, coef_ref, lab_ref, row_ref, plane_ref, level_ref, sums):
    half = own_ref.shape[0]
    box = box_sum(side)
    core = lax.axis_index("core")
    support = channels(sup_ref)
    sup_levels, sup_gains = self_levels(support, box)
    for layer in range(3):
        level_ref[layer] = sup_levels[layer]
    sup_gains = [2.0 * gain for gain in sup_gains]

    def step(image_ref, base, i):
        at = pl.ds(i * CHUNK, CHUNK)
        target = channels(image_ref, at)
        _, tgt_gains = self_levels(target, box)
        level = (WEIGHT_VAR / (9 * CH)) * box(
            sum(s * t for s, t in zip(support, target))
        ) + BIAS_VAR
        gains, corrs = [], []
        for layer in range(3):
            gain = sup_gains[layer] * tgt_gains[layer]
            corr = level * gain
            gains.append(gain)
            corrs.append(corr)
            angle = arcsine(corr)
            if layer < 2:
                level = (WEIGHT_VAR * TWO_PI / 9) * box(angle) + BIAS_VAR
        to = pl.ds(base + i * CHUNK, CHUNK)
        sums[to] = jnp.sum(angle, axis=1)
        grad = (WEIGHT_VAR * TWO_PI / pixels)
        for layer in (2, 1, 0):
            corr = corrs[layer]
            slope = grad * lax.rsqrt((1.0 - corr) * (1.0 + corr))
            plane_ref[to, 1 + layer] = slope * corr
            spread = box(slope * gains[layer])
            if layer > 0:
                grad = (WEIGHT_VAR * TWO_PI / 9) * spread
            else:
                plane_ref[to, 0] = (WEIGHT_VAR / (9 * CH)) * spread

    def both(i, carry):
        step(own_ref, core * half, i)
        step(oth_ref, (1 - core) * half, i)
        return carry

    lax.fori_loop(0, half // CHUNK, both, 0)
    width = row_of["theta"]
    total = lax.dot_general(
        jnp.ones((SUB, LANE), jnp.float32),
        sums[...],
        (((1,), (1,)), ((), ())),
        precision=lax.Precision.HIGHEST,
        preferred_element_type=jnp.float32,
    )
    row_ref[...] = jnp.zeros_like(row_ref)
    row_ref[0:1, 0 : 2 * half] = (WEIGHT_VAR * TWO_PI / pixels) * total[0:1] + BIAS_VAR
    labels = lab_ref.shape[-1]
    own = lax.axis_index("tgt")
    row_ref[0:1, width : width + labels] = coef_ref[pl.ds(own, 1), :]
    row_ref[0:1, width + row_of["class"] : width + row_of["class"] + labels] = lab_ref[...]


def final_body(side, row_of, index_of, all_ref, own_ref, oth_ref, sup_ref, plane_ref, level_ref, grad_ref, res_ref, weight, misfits):
    half = own_ref.shape[0]
    box = box_sum(side)
    core = lax.axis_index("core")
    me = index_of()
    width, classes = row_of["theta"], row_of["class"]
    theta = all_ref[:, 0, 0 : 2 * half]
    coeffs = all_ref[:, 0, width : width + classes]
    labels = all_ref[:, 0, width + classes : width + 2 * classes]
    misfit = (
        lax.dot_general(
            theta,
            coeffs,
            (((0,), (0,)), ((), ())),
            precision=lax.Precision.HIGHEST,
            preferred_element_type=jnp.float32,
        )
        - labels
    )
    own_coeffs = all_ref[me, :, width : width + classes]
    cot = jnp.sum(misfit * own_coeffs, axis=1, keepdims=True)
    misfits[...] = misfit
    res_ref[...] = misfits[pl.ds(me, 1), 0 : res_ref.shape[-1]]
    weight[...] = jnp.broadcast_to(cot, weight.shape)

    def step(image_ref, base, i, carry):
        acc = list(carry)
        for k in range(CHUNK):
            to = base + i * CHUNK + k
            c = weight[pl.ds(to, SUB, stride=0), :]
            target = channels(image_ref, i * CHUNK + k)
            u = c * plane_ref[to, 0]
            for ch in range(CH):
                acc[ch] = acc[ch] + u * target[ch]
            for layer in range(3):
                acc[CH + layer] = acc[CH + layer] + c * plane_ref[to, 1 + layer]
        return tuple(acc)

    def both(i, carry):
        carry = step(own_ref, core * half, i, carry)
        return step(oth_ref, (1 - core) * half, i, carry)

    zero = jnp.zeros((SUB, LANE), jnp.float32)
    acc = lax.fori_loop(0, half // CHUNK, both, (zero,) * (CH + 3))
    carried = None
    for layer in (2, 1, 0):
        level = level_ref[layer]
        inverse = 1.0 / (1.0 + 2.0 * level)
        direct = -inverse * acc[CH + layer]
        if carried is None:
            carried = direct
        else:
            slope = (2.0 * TWO_PI) * inverse * lax.rsqrt(1.0 + 4.0 * level)
            carried = direct + slope * ((WEIGHT_VAR / 9) * box(carried))
    energy = (2.0 * WEIGHT_VAR / (9 * CH)) * box(carried)
    support = channels(sup_ref)
    for ch in range(CH):
        grad = acc[ch] + energy * support[ch]
        for k in range(SUB):
            grad_ref[0, ch : ch + 1, k * LANE : (k + 1) * LANE] = grad[k : k + 1, :]


def local(support, coeffs, targets, labels):
    f32 = jnp.float32
    pixels = support.shape[2]
    side = math.isqrt(pixels)
    chips = lax.axis_size("tgt") * lax.axis_size("row")
    count = 2 * chips
    classes = pl.cdiv(labels.shape[1], LANE) * LANE
    row_of = {"theta": pl.cdiv(count, LANE) * LANE, "class": classes}
    width = row_of["theta"] + 2 * classes

    image = targets.reshape(CH * SUB, LANE)
    own = lax.all_to_all(
        jnp.broadcast_to(image, (chips,) + image.shape), ("tgt", "row"), 0, 0, tiled=True
    )
    oth = lax.ppermute(own, "core", [(0, 1), (1, 0)])
    sup = support.reshape(CH * SUB, LANE)

    row, planes, levels = pl.pallas_call(
        functools.partial(pair_body, side, pixels, row_of),
        out_shape=(
            jax.ShapeDtypeStruct((1, width), f32),
            jax.ShapeDtypeStruct((count, 4, SUB, LANE), f32),
            jax.ShapeDtypeStruct((3, SUB, LANE), f32),
        ),
        scratch_shapes=[pltpu.VMEM((count, LANE), f32)],
        name="pairs",
    )(own, oth, sup, coeffs, labels)

    rows = lax.all_to_all(
        jnp.broadcast_to(row[None], (count, 1, width)), ("core", "tgt", "row"), 0, 0, tiled=True
    )

    def index_of():
        tgt, rows_, core = (lax.axis_index(a) for a in ("tgt", "row", "core"))
        return (core * lax.axis_size("tgt") + tgt) * lax.axis_size("row") + rows_

    grad, residual = pl.pallas_call(
        functools.partial(final_body, side, row_of, index_of),
        out_shape=(
            jax.ShapeDtypeStruct(support.shape, f32),
            jax.ShapeDtypeStruct(labels.shape, f32),
        ),
        scratch_shapes=[pltpu.VMEM((count, LANE), f32), pltpu.VMEM((count, classes), f32)],
        name="final",
    )(rows, own, oth, sup, planes, levels)
    return grad, residual


def solution(mesh):
    tgt, sup = mesh.devices.shape
    chips = Mesh(mesh.devices.reshape(tgt, sup // 2, 2), ("tgt", "row", "core"))
    by_support, by_target = ("row", "core", "tgt"), ("tgt", "row", "core")
    return jax.shard_map(
        local,
        mesh=chips,
        in_specs=(
            P(by_support, None, None),
            P(("row", "core"), None),
            P(by_target, None, None),
            P(by_target, None),
        ),
        out_specs=(P(by_support, None, None), P(by_target, None)),
        check_vma=False,
    )
```

time: 128 us -> 40.7 us (0.32)
  blocking collectives: 65.5 us -> 26.8 us
  other arithmetic: 25.1 us -> 0.02 us
  matrix products: 21.2 us -> 0 us
  local copies, waits for them, and re-layouts: 14.8 us -> 3.42 us
  Pallas kernels: 0 us -> 7.98 us
  waiting for transfers between devices: 0 us -> 1.44 us
    all_gather x3 -> x0, blocking collectives: 32.6 us -> none  [the longest x1 14.3 us: local(): lax.all_gather(targets, 'sup', axis=0, tiled=True)]
    all_to_all x0 -> x2, blocking collectives: none -> 26.8 us  [the longest x1 17.3 us: local(): lax.all_to_all(jnp.broadcast_to(image, (chips,) + image.shape), ('tgt', '...]
    dot_general x4 -> x0, matrix products: 21.2 us -> none  [the longest x2 20.9 us: pair_kernel(): jnp.einsum('scp,tcp->pst', support, targets, precision=lax.Precision.HIGH...]
    psum x1 -> x0, blocking collectives: 16.9 us -> none  [local(): predicted = lax.psum(product(theta.T, coeffs), 'sup')]
    unnamed x1 -> x0, blocking collectives: 16.1 us -> none
    mul x9 -> x0, other arithmetic: 9.21 us -> none  [the longest x2 6 us: pair_kernel(): activated = 2.0 / math.pi * jnp.arcsin(correlation)]
    pallas_call x0 -> x2, Pallas kernels: none -> 7.98 us  [the longest x1 5.26 us: local(): pl.pallas_call(functools.partial(pair_body, side, pixels, row_of), out_sh...]
    div x10 -> x0, other arithmetic: 7.42 us -> none  [the longest x6 6.42 us: spread(): return summed / 9.0]
  transfers between devices with their start and end apart: 0 -> 1, of which waited for: 0 -> 1; matrix products, arithmetic and copies ran while one was open for 0% -> 0% of each run, Pallas kernels for 0% -> 0%
where the time goes in v1:
time: 40.7 us; the launch traced here: 40.3 us
  blocking collectives  26.8 us (66%)
  Pallas kernels  7.98 us (20%)
  local copies, waits for them, and re-layouts  3.42 us (8%)
  waiting for transfers between devices  1.44 us (4%)
  between operations  0.64 us (2%)
    all_to_all x1, blocking collectives, local(): lax.all_to_all(jnp.broadcast_to(image, (chips,) + image.shape), ('tgt', '...  17.3 us
    all_to_all x1, blocking collectives, local(): lax.all_to_all(jnp.broadcast_to(row[None], (count, 1, width)), ('core', '...  9.49 us
    pallas_call x1, Pallas kernels, local(): pl.pallas_call(functools.partial(pair_body, side, pixels, row_of), out_sh...  5.26 us
    pallas_call x1, Pallas kernels, local(): pl.pallas_call(functools.partial(final_body, side, row_of, index_of), out...  2.72 us
    ppermute x1, waiting for transfers between devices, local(): oth = lax.ppermute(own, 'core', [(0, 1), (1, 0)])  1.44 us
    unnamed x6, local copies, waits for them, and re-layouts  1.34 us
    pallas_call x1, local copies, waits for them, and re-layouts, local(): pl.pallas_call(functools.partial(final_body, side, row_of, index_of), out...  1.33 us
  transfers between devices with their start and end apart: 1, of which 1 were waited for; matrix products, arithmetic and copies ran while one was open for 0% of the time, Pallas kernels for 0%

profile of v1, /device:TPU:0, one launch (start us, length us, event | category | flops | bytes accessed | tf_op | source)
XLA Modules:
  0.0 40.3 jit_solution(1741696659713499308)
XLA Ops:
  0.6 0.7 %broadcast_in_dim.11 = f32[16,24,128]{2,1,0:T(8,128)S(1)} broadcast(f32[24,128]{1,0:T(8,128)} %bitcast.4), dimensions={1,2} | broadcast | bytes 208896 | tf_op jit(solution)/shard_map/broadcast_in_dim | solution.py:217
  1.4 17.3 %all_to_all.10.own_ref = f32[16,24,128]{2,1,0:T(8,128)S(1)} all-to-all(f32[16,24,128]{2,1,0:T(8,128)S(1)} %broadcast_in_dim.11), channel_id=1, replica_groups=mesh['tgt'=4,'row'=4,'core'=2] {'tgt','row'}, dimensions={0} | all-to-all | bytes 393216 | tf_op jit(solution)/shard_map/all_to_all | solution.py:216
  18.7 0.0 copy-start
  18.7 0.0 collective-permute-start
  18.7 1.4 %collective-permute-done.oth_ref = f32[16,24,128]{2,1,0:T(8,128)S(1)} collective-permute-done((f32[16,24,128]{2,1,0:T(8,128)S(1)}, f32[16,24,128]{2,1,0:T(8,128)S(1)}, u32[]{:S(2)}, u32[]{:S(2)}) %collective-permute-start) | collective-permute-done | bytes 196640 | tf_op jit(solution)/shard_map/ppermute | solution.py:219
  20.1 0.0 copy-start.1
  20.1 0.0 copy-done
  20.1 0.7 %copy-done.1 = f32[16,24,128]{2,1,0:T(8,128)} copy-done((f32[16,24,128]{2,1,0:T(8,128)}, f32[16,24,128]{2,1,0:T(8,128)S(1)}, u32[]{:S(2)}) %copy-start.1) | copy-done | bytes 196632
  20.8 5.3 %pairs.1 = (f32[1,384]{1,0:T(1,128)}, f32[32,4,8,128]{3,2,1,0:T(8,128)}, f32[3,8,128]{2,1,0:T(8,128)}) custom-call(f32[16,24,128]{2,1,0:T(8,128)} %copy-done, f32[16,24,128]{2,1,0:T(8,128)} %copy-done.1, f32[24,128]{1,0:T(8,128)} %bitcast.2, f32[4,100]{1,0:T(4,128)} %coef_ref.1, f32[1,100]{1,0:T(1,128)} %lab_ref.1), custom_call_target="tpu_custom_call" | custom-call | tf_op jit(solution)/shard_map/pairs/pallas_call | solution.py:222
  26.0 0.0 copy-start.2
  26.0 0.7 %copy-done.2 = f32[1,384]{1,0:T(1,128)S(1)} copy-done((f32[1,384]{1,0:T(1,128)S(1)}, f32[1,384]{1,0:T(1,128)}, u32[]{:S(2)}) %copy-start.2) | copy-done | bytes 1560
  26.8 9.5 %all_to_all.11.all_ref = f32[32,1,384]{2,1,0:T(1,128)} all-to-all(f32[32,1,384]{2,1,0:T(1,128)S(1)} %broadcast_in_dim.13), channel_id=1, replica_groups=mesh['tgt'=4,'row'=4,'core'=2] {'core','tgt','row'}, dimensions={0} | all-to-all | bytes 98304 | tf_op jit(solution)/shard_map/all_to_all | solution.py:233
  36.3 2.7 %final.1 = (f32[1,3,1024]{2,1,0:T(4,128)}, f32[1,100]{1,0:T(1,128)}) custom-call(f32[32,1,384]{2,1,0:T(1,128)} %all_to_all.11.all_ref, f32[16,24,128]{2,1,0:T(8,128)} %copy-done, f32[16,24,128]{2,1,0:T(8,128)} %copy-done.1, f32[24,128]{1,0:T(8,128)} %bitcast.3, f32[32,4,8,128]{3,2,1,0:T(8,128)} %get-tuple-element.6.plane_ref, ...), custom_call_target="tpu_custom_call" | custom-call | tf_op jit(solution)/shard_map/final/pallas_call | solution.py:241
  39.0 1.3 %copy.6 = f32[1,3,1024]{2,0,1:T(1,128)} copy(f32[1,3,1024]{2,1,0:T(4,128)} %get-tuple-element.8) | data formatting | bytes 24576 | tf_op jit(solution)/shard_map/final/pallas_call | solution.py:241
  (2 shorter events, 0.0 us)
Async XLA Ops:
  18.7 1.4 %copy-start = (f32[16,24,128]{2,1,0:T(8,128)}, f32[16,24,128]{2,1,0:T(8,128)S(1)}, u32[]{:S(2)}) copy-start(f32[16,24,128]{2,1,0:T(8,128)S(1)} %all_to_all.10.own_ref) | copy-start | bytes 589828
  18.7 1.4 %collective-permute-start = (f32[16,24,128]{2,1,0:T(8,128)S(1)}, f32[16,24,128]{2,1,0:T(8,128)S(1)}, u32[]{:S(2)}, u32[]{:S(2)}) collective-permute-start(f32[16,24,128]{2,1,0:T(8,128)S(1)} %all_to_all.10.own_ref), channel_id=1, source_target_pairs={{0,1},{1,0},{2,3},{3,2},{4,5},{5,4},{6,7},{7,6},{8,9},{9,8},{10,11... | collective-permute-start | bytes 589832 | tf_op jit(solution)/shard_map/ppermute | solution.py:219
  20.1 0.7 %copy-start.1 = (f32[16,24,128]{2,1,0:T(8,128)}, f32[16,24,128]{2,1,0:T(8,128)S(1)}, u32[]{:S(2)}) copy-start(f32[16,24,128]{2,1,0:T(8,128)S(1)} %collective-permute-done.oth_ref) | copy-start | bytes 589828
  26.0 0.7 %copy-start.2 = (f32[1,384]{1,0:T(1,128)S(1)}, f32[1,384]{1,0:T(1,128)}, u32[]{:S(2)}) copy-start(f32[1,384]{1,0:T(1,128)} %get-tuple-element.5) | copy-start | bytes 4612

commit v2 on v1

--- a/solution.py
+++ b/solution.py
@@ -197,9 +197,7 @@
     energy = (2.0 * WEIGHT_VAR / (9 * CH)) * box(carried)
     support = channels(sup_ref)
     for ch in range(CH):
-        grad = acc[ch] + energy * support[ch]
-        for k in range(SUB):
-            grad_ref[0, ch : ch + 1, k * LANE : (k + 1) * LANE] = grad[k : k + 1, :]
+        grad_ref[ch * SUB : (ch + 1) * SUB, :] = acc[ch] + energy * support[ch]
 
 
 def local(support, coeffs, targets, labels):
@@ -211,6 +209,8 @@
     classes = pl.cdiv(labels.shape[1], LANE) * LANE
     row_of = {"theta": pl.cdiv(count, LANE) * LANE, "class": classes}
     width = row_of["theta"] + 2 * classes
+    vmem = pl.BlockSpec(memory_space=pltpu.VMEM)
+    limit = pltpu.CompilerParams(vmem_limit_bytes=16 * 2**20)
 
     image = targets.reshape(CH * SUB, LANE)
     own = lax.all_to_all(
@@ -226,7 +226,10 @@
             jax.ShapeDtypeStruct((count, 4, SUB, LANE), f32),
             jax.ShapeDtypeStruct((3, SUB, LANE), f32),
         ),
+        in_specs=[vmem] * 5,
+        out_specs=[vmem] * 3,
         scratch_shapes=[pltpu.VMEM((count, LANE), f32)],
+        compiler_params=limit,
         name="pairs",
     )(own, oth, sup, coeffs, labels)
 
@@ -241,13 +244,16 @@
     grad, residual = pl.pallas_call(
         functools.partial(final_body, side, row_of, index_of),
         out_shape=(
-            jax.ShapeDtypeStruct(support.shape, f32),
+            jax.ShapeDtypeStruct(sup.shape, f32),
             jax.ShapeDtypeStruct(labels.shape, f32),
         ),
+        in_specs=[vmem] * 6,
+        out_specs=[vmem] * 2,
         scratch_shapes=[pltpu.VMEM((count, LANE), f32), pltpu.VMEM((count, classes), f32)],
+        compiler_params=limit,
         name="final",
     )(rows, own, oth, sup, planes, levels)
-    return grad, residual
+    return grad.reshape(support.shape), residual
 
 
 def solution(mesh):

time: 40.7 us -> 34.4 us (0.85)
  Pallas kernels: 7.98 us -> 4.97 us
  local copies, waits for them, and re-layouts: 3.42 us -> 0.77 us
  blocking collectives: 26.8 us -> 26.3 us
    pallas_call x1, Pallas kernels: 5.26 us -> 3.55 us  [local(): pl.pallas_call(functools.partial(pair_body, side, pixels, row_of), out_sh...]
    pallas_call x1 -> x0, local copies, waits for them, and re-layouts: 1.33 us -> none  [local(): pl.pallas_call(functools.partial(final_body, side, row_of, index_of), out...]
    unnamed x6, local copies, waits for them, and re-layouts: 1.34 us -> 0.02 us
    pallas_call x1, Pallas kernels: 2.72 us -> 1.41 us  [local(): pl.pallas_call(functools.partial(final_body, side, row_of, index_of), out...]
    all_to_all x1, blocking collectives: 9.49 us -> 8.96 us  [local(): lax.all_to_all(jnp.broadcast_to(row[None], (count, 1, width)), ('core', '...]
where the time goes in v2:
time: 34.4 us; the launch traced here: 34.1 us
  blocking collectives  26.3 us (76%)
  Pallas kernels  4.97 us (14%)
  waiting for transfers between devices  1.44 us (4%)
  local copies, waits for them, and re-layouts  0.77 us (2%)
  between operations  0.67 us (2%)
    all_to_all x1, blocking collectives, local(): lax.all_to_all(jnp.broadcast_to(image, (chips,) + image.shape), ('tgt', '...  17.3 us
    all_to_all x1, blocking collectives, local(): lax.all_to_all(jnp.broadcast_to(row[None], (count, 1, width)), ('core', '...  8.96 us
    pallas_call x1, Pallas kernels, local(): pl.pallas_call(functools.partial(pair_body, side, pixels, row_of), out_sh...  3.55 us
    ppermute x1, waiting for transfers between devices, local(): oth = lax.ppermute(own, 'core', [(0, 1), (1, 0)])  1.44 us
    pallas_call x1, Pallas kernels, local(): pl.pallas_call(functools.partial(final_body, side, row_of, index_of), out...  1.41 us
    broadcast_in_dim x1, local copies, waits for them, and re-layouts, local(): jnp.broadcast_to(image, (chips,) + image.shape)  0.72 us
  transfers between devices with their start and end apart: 1, of which 1 were waited for; matrix products, arithmetic and copies ran while one was open for 0% of the time, Pallas kernels for 0%

profile of v2, /device:TPU:0, one launch (start us, length us, event | category | flops | bytes accessed | tf_op | source)
XLA Modules:
  0.0 34.1 jit_solution(17495532512506322923)
XLA Ops:
  0.6 0.7 %broadcast_in_dim.11 = f32[16,24,128]{2,1,0:T(8,128)S(1)} broadcast(f32[24,128]{1,0:T(8,128)} %bitcast.5), dimensions={1,2} | broadcast | bytes 208896 | tf_op jit(solution)/shard_map/broadcast_in_dim | solution.py:217
  1.4 0.0 copy-start
  1.4 0.0 copy-start.1
  1.4 17.3 %all_to_all.10.own_ref = f32[16,24,128]{2,1,0:T(8,128)S(1)} all-to-all(f32[16,24,128]{2,1,0:T(8,128)S(1)} %broadcast_in_dim.11), channel_id=1, replica_groups=mesh['tgt'=4,'row'=4,'core'=2] {'tgt','row'}, dimensions={0} | all-to-all | bytes 393216 | tf_op jit(solution)/shard_map/all_to_all | solution.py:216
  18.7 0.0 copy-start.2
  18.7 0.0 collective-permute-start
  18.7 1.4 %collective-permute-done.oth_ref = f32[16,24,128]{2,1,0:T(8,128)S(1)} collective-permute-done((f32[16,24,128]{2,1,0:T(8,128)S(1)}, f32[16,24,128]{2,1,0:T(8,128)S(1)}, u32[]{:S(2)}, u32[]{:S(2)}) %collective-permute-start) | collective-permute-done | bytes 196640 | tf_op jit(solution)/shard_map/ppermute | solution.py:219
  20.1 0.0 copy-done
  20.1 0.0 copy-done.1
  20.1 0.0 copy-done.2
  20.1 3.6 %pairs.1 = (f32[1,384]{1,0:T(1,128)S(1)}, f32[32,4,8,128]{3,2,1,0:T(8,128)S(1)}, f32[3,8,128]{2,1,0:T(8,128)S(1)}) custom-call(f32[16,24,128]{2,1,0:T(8,128)S(1)} %all_to_all.10.own_ref, f32[16,24,128]{2,1,0:T(8,128)S(1)} %collective-permute-done.oth_ref, f32[24,128]{1,0:T(8,128)S(1)} %bitcast.3, f32[4,100]{1,0:T(4,128)S(1)} %copy-done.1, f32[1,100]{1,0:T(1,128)S(1)} %copy-done.2), custom_call_target="tpu_custom_call" | custom-call | tf_op jit(solution)/shard_map/pairs/pallas_call | solution.py:222
  23.8 9.0 %all_to_all.11.all_ref = f32[32,1,384]{2,1,0:T(1,128)S(1)} all-to-all(f32[32,1,384]{2,1,0:T(1,128)S(1)} %broadcast_in_dim.13), channel_id=1, replica_groups=mesh['tgt'=4,'row'=4,'core'=2] {'core','tgt','row'}, dimensions={0} | all-to-all | bytes 98304 | tf_op jit(solution)/shard_map/all_to_all | solution.py:236
  32.7 1.4 %final.1 = (f32[24,128]{1,0:T(8,128)}, f32[1,100]{1,0:T(1,128)}) custom-call(f32[32,1,384]{2,1,0:T(1,128)S(1)} %all_to_all.11.all_ref, f32[16,24,128]{2,1,0:T(8,128)S(1)} %all_to_all.10.own_ref, f32[16,24,128]{2,1,0:T(8,128)S(1)} %collective-permute-done.oth_ref, f32[24,128]{1,0:T(8,128)S(1)} %bitcast.4, f32[32,4,8,128]{3,2,1,0:T(8,128)S(1)} %get-tuple-element.8.plane_ref, ...), custom_call_target="tpu_custom_call" | custom-call | tf_op jit(solution)/shard_map/final/pallas_call | solution.py:244
  (2 shorter events, 0.1 us)
Async XLA Ops:
  1.4 18.8 %copy-start = (f32[1,3,1024]{2,0,1:T(1,128)S(1)}, f32[1,3,1024]{2,0,1:T(1,128)}, u32[]{:S(2)}) copy-start(f32[1,3,1024]{2,0,1:T(1,128)} %param.4) | copy-start | bytes 36868
  1.4 18.8 %copy-start.1 = (f32[4,100]{1,0:T(4,128)S(1)}, f32[4,100]{1,0:T(4,128)}, u32[]{:S(2)}) copy-start(f32[4,100]{1,0:T(4,128)} %coef_ref.1) | copy-start | bytes 4804
  18.7 1.5 %copy-start.2 = (f32[1,100]{1,0:T(1,128)S(1)}, f32[1,100]{1,0:T(1,128)}, u32[]{:S(2)}) copy-start(f32[1,100]{1,0:T(1,128)} %lab_ref.1) | copy-start | bytes 1204
  18.7 1.4 %collective-permute-start = (f32[16,24,128]{2,1,0:T(8,128)S(1)}, f32[16,24,128]{2,1,0:T(8,128)S(1)}, u32[]{:S(2)}, u32[]{:S(2)}) collective-permute-start(f32[16,24,128]{2,1,0:T(8,128)S(1)} %all_to_all.10.own_ref), channel_id=1, source_target_pairs={{0,1},{1,0},{2,3},{3,2},{4,5},{5,4},{6,7},{7,6},{8,9},{9,8},{10,11... | collective-permute-start | bytes 589832 | tf_op jit(solution)/shard_map/ppermute | solution.py:219

commit v3 on v0

v3 whole, which is shorter than its diff:
```python
import functools
import math

import jax
import jax.numpy as jnp
from jax import lax
from jax.experimental import pallas as pl
from jax.experimental.pallas import tpu as pltpu
from jax.sharding import Mesh
from jax.sharding import PartitionSpec as P

WEIGHT_VAR = 1.6
BIAS_VAR = 0.1
DEPTH = 3
CH = 3
SUB = 8
LANE = 128
TWO_PI = 2.0 / math.pi
FIRST = WEIGHT_VAR / (9 * CH)
LATER = WEIGHT_VAR * TWO_PI / 9

NEAR = (1.6666752422e-1, 7.4953002686e-2, 4.5470025998e-2, 2.4181311049e-2, 4.2163199048e-2)
WIDE = (
    0.16666266322135925,
    0.07520359754562378,
    0.04114901274442673,
    0.058932434767484665,
    -0.10370756685733795,
    0.3290194272994995,
    -0.39874982833862305,
    0.2500518262386322,
)


def horner(z, coefficients):
    result = coefficients[-1]
    for value in coefficients[-2::-1]:
        result = result * z + value
    return result


def arcsine(x):
    a = jnp.abs(x)
    large, negative = a > 0.5, x < 0.0
    rest = jnp.maximum(2.0 - 2.0 * a, 1e-30)
    z = jnp.where(large, 0.25 * rest, x * x)
    root = rest * lax.rsqrt(rest)
    t = jnp.where(large, jnp.where(negative, root, -root), x)
    offset = jnp.where(large, jnp.where(negative, -0.5 * math.pi, 0.5 * math.pi), 0.0)
    return offset + (t + (t * z) * horner(z, NEAR))


def arcsine_inner(x):
    z = x * x
    return x + (x * z) * horner(z, WIDE)


class Grid:
    def __init__(self, side):
        lane = lax.broadcasted_iota(jnp.int32, (SUB, LANE), 1)
        sub = lax.broadcasted_iota(jnp.int32, (SUB, LANE), 0)
        self.side, self.fold = side, LANE // side
        column = lane % side
        self.place = lane // side
        self.not_left, self.not_right = column != 0, column != side - 1
        self.not_top, self.not_bottom = sub != 0, sub != SUB - 1

    def swap(self, arrays):
        arrays, step = list(arrays), 1
        while step < self.fold:
            low = (self.place // step) % 2 == 0
            shift = step * self.side
            for i in range(self.fold):
                if i & step == 0:
                    a, b = arrays[i], arrays[i + step]
                    axis = a.ndim - 1
                    arrays[i] = jnp.where(low, a, pltpu.roll(b, shift, axis))
                    arrays[i + step] = jnp.where(low, pltpu.roll(a, LANE - shift, axis), b)
            step *= 2
        return arrays

    def box(self, rows):
        h = []
        for x in rows:
            axis = x.ndim - 1
            h.append(
                x
                + jnp.where(self.not_left, pltpu.roll(x, 1, axis), 0.0)
                + jnp.where(self.not_right, pltpu.roll(x, LANE - 1, axis), 0.0)
            )
        axis = rows[0].ndim - 2
        above = jnp.where(self.not_top, pltpu.roll(h[-1], 1, axis), 0.0)
        below = jnp.where(self.not_bottom, pltpu.roll(h[0], SUB - 1, axis), 0.0)
        ring = [above] + h + [below]
        pairs = [ring[k] + ring[k + 1] for k in range(0, len(ring), 2)]
        out = []
        for q in range(self.fold):
            if q % 2 == 0:
                out.append(pairs[q // 2] + ring[q + 2])
            else:
                out.append(ring[q] + pairs[(q + 1) // 2])
        return out


def affine(factor, rows):
    return [factor * x + BIAS_VAR for x in rows]


def self_levels(grid, image):
    energy = [sum(x * x for x in rows) for rows in zip(*image)]
    level = affine(FIRST, grid.box(energy))
    levels, gains = [], []
    for layer in range(DEPTH):
        gain = [lax.rsqrt(1.0 + 2.0 * x) for x in level]
        levels.append(level)
        gains.append(gain)
        if layer + 1 < DEPTH:
            inner = [(2.0 * x) * (g * g) for x, g in zip(level, gain)]
            angle = [(arcsine if layer == 0 else arcsine_inner)(x) for x in inner]
            level = affine(LATER, grid.box(angle))
    return levels, gains


def pairs_of(grid, pixels, block, image_ref, state, plane_ref, sum_of):
    support, gains2, decay, slope_of = state
    fold = grid.fold

    def step(k, carry):
        at = pl.ds(k * block, block)
        to = pl.ds(k * (block // fold), block // fold)
        target = []
        for c in range(CH):
            x = image_ref[at, c * SUB : (c + 1) * SUB, :].reshape(block // fold, fold, SUB, LANE)
            target.append(grid.swap([x[:, i] for i in range(fold)]))
        _, tgt_gains = self_levels(grid, target)
        level = [
            sum(s * t for s, t in zip(row_s, row_t))
            for row_s, row_t in zip(zip(*support), zip(*target))
        ]
        level = affine(FIRST, grid.box(level))
        gains, corrs = [], []
        for layer in range(DEPTH):
            gain = [s * t for s, t in zip(gains2[layer], tgt_gains[layer])]
            corr = [x * g for x, g in zip(level, gain)]
            gains.append(gain)
            corrs.append(corr)
            angle = [(arcsine if layer == 0 else arcsine_inner)(x) for x in corr]
            if layer + 1 < DEPTH:
                level = affine(LATER, grid.box(angle))
        sum_of(k, jnp.sum(sum(angle), axis=1))
        grad = [WEIGHT_VAR * TWO_PI / pixels] * fold
        carried = None
        for layer in range(DEPTH - 1, -1, -1):
            slope = [
                g * lax.rsqrt((1.0 - x) * (1.0 + x)) for g, x in zip(grad, corrs[layer])
            ]
            direct = [d * (s * x) for d, s, x in zip(decay[layer], slope, corrs[layer])]
            if carried is None:
                carried = direct
            else:
                back = grid.box(carried)
                carried = [d + m * x for d, m, x in zip(direct, slope_of[layer], back)]
            factor = LATER if layer > 0 else FIRST
            grad = [
                factor * x for x in grid.box([s * g for s, g in zip(slope, gains[layer])])
            ]
        energy = [(2.0 * FIRST) * x for x in grid.box(carried)]
        for c in range(CH):
            for q in range(fold):
                plane_ref[to, c, q] = grad[q] * target[c][q] + energy[q] * support[c][q]
        return carry

    lax.fori_loop(0, image_ref.shape[0] // block, step, 0)


def first_body(
    classes, tgt_hbm, sup_hbm, coef_hbm, lab_hbm,
    image_ref, sup_ref, head_ref, tgt_ref, coef_ref, lab_ref, sems,
):
    pairs = ((tgt_hbm, tgt_ref), (sup_hbm, sup_ref), (coef_hbm, coef_ref), (lab_hbm, lab_ref))
    copies = [pltpu.make_async_copy(a, b, sems.at[k]) for k, (a, b) in enumerate(pairs)]
    for copy in copies:
        copy.start()
    head_ref[...] = jnp.zeros_like(head_ref)
    copies[0].wait()
    image = tgt_ref[...]
    for k in range(image_ref.shape[0]):
        image_ref[k] = image
    for copy in copies[1:]:
        copy.wait()
    labels = lab_ref.shape[-1]
    head_ref[0:1, 0:labels] = coef_ref[pl.ds(lax.axis_index("tgt"), 1), :]
    head_ref[0:1, classes : classes + labels] = lab_ref[...]


def own_body(side, pixels, block, own_ref, sup_ref, sum_ref, plane_ref, state_ref):
    grid = Grid(side)
    support = [
        grid.swap([sup_ref[c * SUB : (c + 1) * SUB, :]] * grid.fold) for c in range(CH)
    ]
    levels, gains = self_levels(grid, support)
    gains2, decay, slope_of = [], [], []
    for level, gain in zip(levels, gains):
        gains2.append([2.0 * g for g in gain])
        decay.append([-(g * g) for g in gain])
        slope_of.append(
            [(2.0 * LATER) * (g * g) * lax.rsqrt(1.0 + 4.0 * x) for x, g in zip(level, gain)]
        )
    state = (support, gains2, decay, slope_of)
    for part, arrays in enumerate(state):
        for layer in range(DEPTH):
            for q in range(grid.fold):
                state_ref[part, layer, q] = arrays[layer][q]

    def sum_of(k, rows):
        for g in range(rows.shape[0]):
            sum_ref[pl.ds(k * rows.shape[0] + g, 1)] = rows[g : g + 1]

    pairs_of(grid, pixels, block, own_ref, state, plane_ref, sum_of)


def other_body(
    side, pixels, block, width, oth_ref, state_ref, own_sum_ref, head_ref,
    row_ref, plane_ref, sums,
):
    grid = Grid(side)
    half = oth_ref.shape[0]
    groups = half // grid.fold
    core = lax.axis_index("core")
    for g in range(groups):
        sums[pl.ds(core * groups + g, 1)] = own_sum_ref[g : g + 1]
    state = [
        [[state_ref[part, layer, q] for q in range(grid.fold)] for layer in range(DEPTH)]
        for part in range(4)
    ]

    def sum_of(k, rows):
        base = (1 - core) * groups + k * rows.shape[0]
        for g in range(rows.shape[0]):
            sums[pl.ds(base + g, 1)] = rows[g : g + 1]

    pairs_of(grid, pixels, block, oth_ref, state, plane_ref, sum_of)

    count = 2 * half
    lane = lax.broadcasted_iota(jnp.int32, (LANE, count), 0)
    image = lax.broadcasted_iota(jnp.int32, (LANE, count), 1)
    select = jnp.where(lane // side == image % grid.fold, 1.0, 0.0)
    total = lax.dot_general(
        sums[...],
        select,
        (((1,), (0,)), ((), ())),
        precision=lax.Precision.HIGHEST,
        preferred_element_type=jnp.float32,
    )
    group = lax.broadcasted_iota(jnp.int32, total.shape, 0)
    image = lax.broadcasted_iota(jnp.int32, total.shape, 1)
    total = jnp.sum(
        jnp.where(image // grid.fold == group, total, 0.0), axis=0, keepdims=True
    )
    row_ref[:, 0:width] = jnp.zeros((1, width), jnp.float32)
    row_ref[:, 0:count] = (WEIGHT_VAR * TWO_PI / pixels) * total + BIAS_VAR
    row_ref[:, width:] = head_ref[...]


def final_body(
    side, row_of, index_of, all_ref, plane0_ref, plane1_ref, grad_ref, res_ref,
    weight, group_weight, misfits,
):
    grid = Grid(side)
    fold = grid.fold
    groups = plane0_ref.shape[0]
    count = 2 * groups * fold
    core = lax.axis_index("core")
    me = index_of()
    width, classes = row_of["theta"], row_of["class"]
    theta = all_ref[:, 0, 0:count]
    coeffs = all_ref[:, 0, width : width + classes]
    labels = all_ref[:, 0, width + classes : width + 2 * classes]
    misfit = (
        lax.dot_general(
            theta,
            coeffs,
            (((0,), (0,)), ((), ())),
            precision=lax.Precision.HIGHEST,
            preferred_element_type=jnp.float32,
        )
        - labels
    )
    own_coeffs = all_ref[me, :, width : width + classes]
    cot = jnp.sum(misfit * own_coeffs, axis=1, keepdims=True)
    weight[...] = jnp.broadcast_to(cot, weight.shape)
    place = lax.broadcasted_iota(jnp.int32, group_weight.shape, 1) // side
    rows = weight[pl.ds(0, 2 * groups, stride=fold), :]
    for i in range(1, fold):
        rows = jnp.where(place == i, weight[pl.ds(i, 2 * groups, stride=fold), :], rows)
    group_weight[...] = rows
    misfits[...] = misfit
    res_ref[...] = misfits[pl.ds(me, 1), 0 : res_ref.shape[-1]]

    block = math.gcd(groups, 4)

    def step(plane_ref, base, k, acc):
        acc = list(acc)
        for g in range(block):
            c = group_weight[pl.ds(base + k * block + g, SUB, stride=0), :]
            for n in range(CH * fold):
                acc[n] = acc[n] + c * plane_ref[k * block + g, n // fold, n % fold]
        return acc

    def both(k, acc):
        acc = step(plane0_ref, core * groups, k, acc)
        return tuple(step(plane1_ref, (1 - core) * groups, k, acc))

    zero = jnp.zeros((SUB, LANE), jnp.float32)
    acc = lax.fori_loop(0, groups // block, both, (zero,) * (CH * fold))
    for c in range(CH):
        out = None
        for q in range(fold):
            x, shift = acc[c * fold + q], LANE // 2
            while shift >= side:
                x = x + pltpu.roll(x, shift, 1)
                shift //= 2
            out = x if out is None else jnp.where(grid.place == q, x, out)
        grad_ref[c * SUB : (c + 1) * SUB, :] = out


def local(support, coeffs, targets, labels):
    f32 = jnp.float32
    pixels = support.shape[2]
    side = math.isqrt(pixels)
    fold = LANE // side
    chips = lax.axis_size("tgt") * lax.axis_size("row")
    count = 2 * chips
    classes = pl.cdiv(labels.shape[1], LANE) * LANE
    row_of = {"theta": pl.cdiv(count, LANE) * LANE, "class": classes}
    width = row_of["theta"] + 2 * classes
    block = math.gcd(chips, 4 * fold)
    groups = chips // fold
    assert support.shape[0] == 1 and targets.shape[0] == 1
    assert side * side == pixels == SUB * LANE and groups * fold == chips

    vmem = pl.BlockSpec(memory_space=pltpu.VMEM)
    hbm = pl.BlockSpec(memory_space=pltpu.HBM)
    limit = pltpu.CompilerParams(vmem_limit_bytes=16 * 2**20)
    effort = pl.CostEstimate(
        flops=300 * chips * pixels, bytes_accessed=24 * chips * pixels, transcendentals=0
    )

    sup_shape = (CH * SUB, LANE)
    inputs = (targets.reshape(sup_shape), support.reshape(sup_shape), coeffs, labels)
    images, sup, head = pl.pallas_call(
        functools.partial(first_body, classes),
        out_shape=(
            jax.ShapeDtypeStruct((chips,) + sup_shape, f32),
            jax.ShapeDtypeStruct(sup_shape, f32),
            jax.ShapeDtypeStruct((1, 2 * classes), f32),
        ),
        in_specs=[hbm] * 4,
        out_specs=[vmem] * 3,
        scratch_shapes=[
            pltpu.VMEM(sup_shape, f32),
            pltpu.VMEM(coeffs.shape, f32),
            pltpu.VMEM(labels.shape, f32),
            pltpu.SemaphoreType.DMA((4,)),
        ],
        compiler_params=limit,
        name="first",
    )(*(pltpu.with_memory_space_constraint(x, pltpu.HBM) for x in inputs))
    own = lax.all_to_all(images, ("tgt", "row"), 0, 0, tiled=True)
    oth = lax.ppermute(own, "core", [(0, 1), (1, 0)])

    planes = jax.ShapeDtypeStruct((groups, CH, fold, SUB, LANE), f32)
    sums, planes0, state = pl.pallas_call(
        functools.partial(own_body, side, pixels, block),
        out_shape=(
            jax.ShapeDtypeStruct((groups, LANE), f32),
            planes,
            jax.ShapeDtypeStruct((4, DEPTH, fold, SUB, LANE), f32),
        ),
        in_specs=[vmem] * 2,
        out_specs=[vmem] * 3,
        compiler_params=limit,
        cost_estimate=effort,
        name="own",
    )(own, sup)
    row, planes1 = pl.pallas_call(
        functools.partial(other_body, side, pixels, block, row_of["theta"]),
        out_shape=(jax.ShapeDtypeStruct((1, width), f32), planes),
        in_specs=[vmem] * 4,
        out_specs=[vmem] * 2,
        scratch_shapes=[pltpu.VMEM((2 * groups, LANE), f32)],
        compiler_params=limit,
        cost_estimate=effort,
        name="other",
    )(oth, state, sums, head)

    rows = lax.all_to_all(
        jnp.broadcast_to(row[None], (count, 1, width)), ("core", "tgt", "row"), 0, 0, tiled=True
    )

    def index_of():
        tgt, place, core = (lax.axis_index(a) for a in ("tgt", "row", "core"))
        return (core * lax.axis_size("tgt") + tgt) * lax.axis_size("row") + place

    grad, residual = pl.pallas_call(
        functools.partial(final_body, side, row_of, index_of),
        out_shape=(
            jax.ShapeDtypeStruct(sup.shape, f32),
            jax.ShapeDtypeStruct(labels.shape, f32),
        ),
        in_specs=[vmem] * 3,
        out_specs=[vmem] * 2,
        scratch_shapes=[
            pltpu.VMEM((count, LANE), f32),
            pltpu.VMEM((2 * groups, LANE), f32),
            pltpu.VMEM((count, classes), f32),
        ],
        compiler_params=limit,
        name="final",
    )(rows, planes0, planes1)
    return grad.reshape(support.shape), residual


def solution(mesh):
    tgt, sup = mesh.devices.shape
    chips = Mesh(mesh.devices.reshape(tgt, sup // 2, 2), ("tgt", "row", "core"))
    by_support, by_target = ("row", "core", "tgt"), ("tgt", "row", "core")
    return jax.shard_map(
        local,
        mesh=chips,
        in_specs=(
            P(by_support, None, None),
            P(("row", "core"), None),
            P(by_target, None, None),
            P(by_target, None),
        ),
        out_specs=(P(by_support, None, None), P(by_target, None)),
        check_vma=False,
    )
```

time: 128 us -> 31.7 us (0.25)
  blocking collectives: 65.5 us -> 26.3 us
  other arithmetic: 25.1 us -> 0.02 us
  matrix products: 21.2 us -> 0 us
  local copies, waits for them, and re-layouts: 14.8 us -> 0.03 us
  Pallas kernels: 0 us -> 4.12 us
    all_gather x3 -> x0, blocking collectives: 32.6 us -> none  [the longest x1 14.3 us: local(): lax.all_gather(targets, 'sup', axis=0, tiled=True)]
    all_to_all x0 -> x2, blocking collectives: none -> 26.3 us  [the longest x1 17.3 us: local(): own = lax.all_to_all(images, ('tgt', 'row'), 0, 0, tiled=True)]
    dot_general x4 -> x0, matrix products: 21.2 us -> none  [the longest x2 20.9 us: pair_kernel(): jnp.einsum('scp,tcp->pst', support, targets, precision=lax.Precision.HIGH...]
    psum x1 -> x0, blocking collectives: 16.9 us -> none  [local(): predicted = lax.psum(product(theta.T, coeffs), 'sup')]
    unnamed x1 -> x0, blocking collectives: 16.1 us -> none
    mul x9 -> x0, other arithmetic: 9.21 us -> none  [the longest x2 6 us: pair_kernel(): activated = 2.0 / math.pi * jnp.arcsin(correlation)]
    div x10 -> x0, other arithmetic: 7.42 us -> none  [the longest x6 6.42 us: spread(): return summed / 9.0]
    reduce_sum x6 -> x0, other arithmetic: 5.39 us -> none  [the longest x3 3.02 us: pair_kernel(): 2.0 * kernel_level.reshape(SIDE, SIDE, sup_count, tgt_count)]
  transfers between devices with their start and end apart: 0 -> 1, of which waited for: 0 -> 1; matrix products, arithmetic and copies ran while one was open for 0% -> 0% of each run, Pallas kernels for 0% -> 4%
where the time goes in v3:
time: 31.7 us; the launch traced here: 31.4 us
  blocking collectives  26.3 us (83%)
  Pallas kernels  4.12 us (13%)
  between operations  0.66 us (2%)
    all_to_all x1, blocking collectives, local(): own = lax.all_to_all(images, ('tgt', 'row'), 0, 0, tiled=True)  17.3 us
    all_to_all x1, blocking collectives, local(): lax.all_to_all(jnp.broadcast_to(row[None], (count, 1, width)), ('core', '...  8.96 us
    pallas_call x1, Pallas kernels, local(): pl.pallas_call(functools.partial(own_body, side, pixels, block), out_shap...  1.16 us
    pallas_call x1, Pallas kernels, local(): pl.pallas_call(functools.partial(other_body, side, pixels, block, row_of[...  1.12 us
    pallas_call x1, Pallas kernels, local(): pl.pallas_call(functools.partial(final_body, side, row_of, index_of), out...  1.08 us
    pallas_call x1, Pallas kernels, local(): pl.pallas_call(functools.partial(first_body, classes), out_shape=(jax.Sha...  0.77 us
  transfers between devices with their start and end apart: 1, of which 1 were waited for; matrix products, arithmetic and copies ran while one was open for 0% of the time, Pallas kernels for 4%

profile of v3, /device:TPU:0, one launch (start us, length us, event | category | flops | bytes accessed | tf_op | source)
XLA Modules:
  0.0 31.4 jit_solution(12877481060737723620)
XLA Ops:
  0.6 0.8 %first.1 = (f32[16,24,128]{2,1,0:T(8,128)S(1)}, f32[24,128]{1,0:T(8,128)S(1)}, f32[1,256]{1,0:T(1,128)S(1)}) custom-call(f32[24,128]{1,0:T(8,128)} %bitcast.3, f32[24,128]{1,0:T(8,128)} %bitcast.4, f32[4,100]{1,0:T(4,128)} %coef_hbm.1, f32[1,100]{1,0:T(1,128)} %lab_hbm.1), custom_call_target="tpu_custom_call" | custom-call | tf_op jit(solution)/shard_map/first/pallas_call | solution.py:351
  1.4 17.3 %all_to_all.10.own_ref = f32[16,24,128]{2,1,0:T(8,128)S(1)} all-to-all(f32[16,24,128]{2,1,0:T(8,128)S(1)} %get-tuple-element.12), channel_id=1, replica_groups=mesh['tgt'=4,'row'=4,'core'=2] {'tgt','row'}, dimensions={0} | all-to-all | bytes 393216 | tf_op jit(solution)/shard_map/all_to_all | solution.py:369
  18.7 0.0 collective-permute-start
  18.7 1.2 %own.1 = (f32[4,128]{1,0:T(4,128)S(1)}, f32[4,3,4,8,128]{4,3,2,1,0:T(8,128)S(1)}, f32[4,3,4,8,128]{4,3,2,1,0:T(8,128)S(1)}) custom-call(f32[16,24,128]{2,1,0:T(8,128)S(1)} %all_to_all.10.own_ref, f32[24,128]{1,0:T(8,128)S(1)} %get-tuple-element.13.sup_ref), custom_call_target="tpu_custom_call" | custom-call | flops 4915200 | bytes 393216 | tf_op jit(solution)/shard_map/own/pallas_call | solution.py:373
  19.9 0.3 collective-permute-done.oth_ref
  20.2 1.1 %other.1 = (f32[1,384]{1,0:T(1,128)S(1)}, f32[4,3,4,8,128]{4,3,2,1,0:T(8,128)S(1)}) custom-call(f32[16,24,128]{2,1,0:T(8,128)S(1)} %collective-permute-done.oth_ref, f32[4,3,4,8,128]{4,3,2,1,0:T(8,128)S(1)} %get-tuple-element.14.state_ref, f32[4,128]{1,0:T(4,128)S(1)} %get-tuple-element.15.own_sum_ref, f32[1,256]{1,0:T(1,128)S(1)} %get-tuple-element.16.head_ref), custom_call_target="tpu_custom_call" | custom-call | flops 4915200 | bytes 393216 | tf_op jit(solution)/shard_map/other/pallas_call | solution.py:386
  21.3 9.0 %all_to_all.11.all_ref = f32[32,1,384]{2,1,0:T(1,128)S(1)} all-to-all(f32[32,1,384]{2,1,0:T(1,128)S(1)} %broadcast_in_dim.9), channel_id=1, replica_groups=mesh['tgt'=4,'row'=4,'core'=2] {'core','tgt','row'}, dimensions={0} | all-to-all | bytes 98304 | tf_op jit(solution)/shard_map/all_to_all | solution.py:397
  30.3 1.1 %final.1 = (f32[24,128]{1,0:T(8,128)}, f32[1,100]{1,0:T(1,128)}) custom-call(f32[32,1,384]{2,1,0:T(1,128)S(1)} %all_to_all.11.all_ref, f32[4,3,4,8,128]{4,3,2,1,0:T(8,128)S(1)} %get-tuple-element.18.plane0_ref, f32[4,3,4,8,128]{4,3,2,1,0:T(8,128)S(1)} %get-tuple-element.19.plane1_ref), custom_call_target="tpu_custom_call" | custom-call | tf_op jit(solution)/shard_map/final/pallas_call | solution.py:405
  (2 shorter events, 0.1 us)
Async XLA Ops:
  18.7 1.4 %collective-permute-start = (f32[16,24,128]{2,1,0:T(8,128)S(1)}, f32[16,24,128]{2,1,0:T(8,128)S(1)}, u32[]{:S(2)}, u32[]{:S(2)}) collective-permute-start(f32[16,24,128]{2,1,0:T(8,128)S(1)} %all_to_all.10.own_ref), channel_id=1, source_target_pairs={{0,1},{1,0},{2,3},{3,2},{4,5},{5,4},{6,7},{7,6},{8,9},{9,8},{10,11... | collective-permute-start | bytes 589832 | tf_op jit(solution)/shard_map/ppermute | solution.py:370

commit v4 on v3

--- a/solution.py
+++ b/solution.py
@@ -16,11 +16,13 @@
 SUB = 8
 LANE = 128
 TWO_PI = 2.0 / math.pi
+PARTS = 5
 FIRST = WEIGHT_VAR / (9 * CH)
 LATER = WEIGHT_VAR * TWO_PI / 9
 
 NEAR = (1.6666752422e-1, 7.4953002686e-2, 4.5470025998e-2, 2.4181311049e-2, 4.2163199048e-2)
 WIDE = (
+    1.0,
     0.16666266322135925,
     0.07520359754562378,
     0.04114901274442673,
@@ -30,29 +32,39 @@
     -0.39874982833862305,
     0.2500518262386322,
 )
-
-
-def horner(z, coefficients):
-    result = coefficients[-1]
+HALF = (
+    1.0000000202678234,
+    0.1666621810142767,
+    0.07516158417922122,
+    0.042482407794996346,
+    0.04384003568012658,
+    -0.018689176226557736,
+    0.07216594689625302,
+)
+
+
+def horner(z, coefficients, scale=1.0):
+    result = scale * coefficients[-1]
     for value in coefficients[-2::-1]:
-        result = result * z + value
+        result = result * z + scale * value
     return result
 
 
 def arcsine(x):
     a = jnp.abs(x)
     large, negative = a > 0.5, x < 0.0
-    rest = jnp.maximum(2.0 - 2.0 * a, 1e-30)
-    z = jnp.where(large, 0.25 * rest, x * x)
-    root = rest * lax.rsqrt(rest)
+    left = 1.0 - a
+    z = jnp.where(large, 0.5 * left, x * x)
+    root = (2.0 * left) * lax.rsqrt(2.0 * left)
     t = jnp.where(large, jnp.where(negative, root, -root), x)
-    offset = jnp.where(large, jnp.where(negative, -0.5 * math.pi, 0.5 * math.pi), 0.0)
-    return offset + (t + (t * z) * horner(z, NEAR))
-
-
-def arcsine_inner(x):
+    right = LATER * 0.5 * math.pi
+    offset = jnp.where(large, jnp.where(negative, -right, right), 0.0)
+    return offset + t * (LATER + z * horner(z, NEAR, LATER)), left * (1.0 + a)
+
+
+def arcsine_inner(x, scale):
     z = x * x
-    return x + (x * z) * horner(z, WIDE)
+    return x * horner(z, WIDE, scale), 1.0 - z
 
 
 class Grid:
@@ -64,6 +76,13 @@
         self.place = lane // side
         self.not_left, self.not_right = column != 0, column != side - 1
         self.not_top, self.not_bottom = sub != 0, sub != SUB - 1
+
+    def neighbours(self):
+        across = jnp.where(self.not_left, 1.0, 0.0) + jnp.where(self.not_right, 2.0, 1.0)
+        rows = [across * 3.0] * self.fold
+        rows[0] = across * jnp.where(self.not_top, 3.0, 2.0)
+        rows[-1] = across * jnp.where(self.not_bottom, 3.0, 2.0)
+        return rows
 
     def swap(self, arrays):
         arrays, step = list(arrays), 1
@@ -102,27 +121,22 @@
         return out
 
 
-def affine(factor, rows):
-    return [factor * x + BIAS_VAR for x in rows]
-
-
-def self_levels(grid, image):
+def self_gains(grid, image):
     energy = [sum(x * x for x in rows) for rows in zip(*image)]
-    level = affine(FIRST, grid.box(energy))
-    levels, gains = [], []
-    for layer in range(DEPTH):
-        gain = [lax.rsqrt(1.0 + 2.0 * x) for x in level]
-        levels.append(level)
+    start = 1.0 + 2.0 * BIAS_VAR
+    gain = [lax.rsqrt((2.0 * FIRST) * x + start) for x in grid.box(energy)]
+    gains = [gain]
+    most = [(LATER * math.pi) * n + start for n in grid.neighbours()]
+    powers = [c * 0.5**k for k, c in enumerate(HALF)]
+    for _ in range(DEPTH - 1):
+        less = [g * horner(g * g, powers, 4.0 * LATER * math.sqrt(0.5)) for g in gain]
+        gain = [lax.rsqrt(m - x) for m, x in zip(most, grid.box(less))]
         gains.append(gain)
-        if layer + 1 < DEPTH:
-            inner = [(2.0 * x) * (g * g) for x, g in zip(level, gain)]
-            angle = [(arcsine if layer == 0 else arcsine_inner)(x) for x in inner]
-            level = affine(LATER, grid.box(angle))
-    return levels, gains
-
-
-def pairs_of(grid, pixels, block, image_ref, state, plane_ref, sum_of):
-    support, gains2, decay, slope_of = state
+    return gains
+
+
+def pairs_of(grid, block, image_ref, state, plane_ref, sum_of):
+    scaled, double, gains2, decay, slope_of = state
     fold = grid.fold
 
     def step(k, carry):
@@ -132,42 +146,45 @@
         for c in range(CH):
             x = image_ref[at, c * SUB : (c + 1) * SUB, :].reshape(block // fold, fold, SUB, LANE)
             target.append(grid.swap([x[:, i] for i in range(fold)]))
-        _, tgt_gains = self_levels(grid, target)
-        level = [
-            sum(s * t for s, t in zip(row_s, row_t))
-            for row_s, row_t in zip(zip(*support), zip(*target))
-        ]
-        level = affine(FIRST, grid.box(level))
-        gains, corrs = [], []
+        tgt_gains = self_gains(grid, target)
+        spread = grid.box(
+            [
+                sum(s * t for s, t in zip(row_s, row_t))
+                for row_s, row_t in zip(zip(*scaled), zip(*target))
+            ]
+        )
+        gains, corrs, rests = [], [], []
         for layer in range(DEPTH):
             gain = [s * t for s, t in zip(gains2[layer], tgt_gains[layer])]
-            corr = [x * g for x, g in zip(level, gain)]
+            corr = [(x + BIAS_VAR) * g for x, g in zip(spread, gain)]
+            if layer == 0:
+                both = [arcsine(x) for x in corr]
+            else:
+                scale = LATER if layer + 1 < DEPTH else 1.0
+                both = [arcsine_inner(x, scale) for x in corr]
+            angle = [x for x, _ in both]
             gains.append(gain)
             corrs.append(corr)
-            angle = [(arcsine if layer == 0 else arcsine_inner)(x) for x in corr]
+            rests.append([x for _, x in both])
             if layer + 1 < DEPTH:
-                level = affine(LATER, grid.box(angle))
+                spread = grid.box(angle)
         sum_of(k, jnp.sum(sum(angle), axis=1))
-        grad = [WEIGHT_VAR * TWO_PI / pixels] * fold
-        carried = None
-        for layer in range(DEPTH - 1, -1, -1):
-            slope = [
-                g * lax.rsqrt((1.0 - x) * (1.0 + x)) for g, x in zip(grad, corrs[layer])
+        slope = [lax.rsqrt(x) for x in rests[-1]]
+        carried = [d * (s * x) for d, s, x in zip(decay[-1], slope, corrs[-1])]
+        for layer in range(DEPTH - 2, -1, -1):
+            grad = grid.box([s * g for s, g in zip(slope, gains[layer + 1])])
+            slope = [g * lax.rsqrt(x) for g, x in zip(grad, rests[layer])]
+            carried = [
+                d * (s * x) + m * y
+                for d, s, x, m, y in zip(
+                    decay[layer], slope, corrs[layer], slope_of[layer], grid.box(carried)
+                )
             ]
-            direct = [d * (s * x) for d, s, x in zip(decay[layer], slope, corrs[layer])]
-            if carried is None:
-                carried = direct
-            else:
-                back = grid.box(carried)
-                carried = [d + m * x for d, m, x in zip(direct, slope_of[layer], back)]
-            factor = LATER if layer > 0 else FIRST
-            grad = [
-                factor * x for x in grid.box([s * g for s, g in zip(slope, gains[layer])])
-            ]
-        energy = [(2.0 * FIRST) * x for x in grid.box(carried)]
+        grad = grid.box([s * g for s, g in zip(slope, gains[0])])
+        energy = grid.box(carried)
         for c in range(CH):
             for q in range(fold):
-                plane_ref[to, c, q] = grad[q] * target[c][q] + energy[q] * support[c][q]
+                plane_ref[to, c, q] = grad[q] * target[c][q] + energy[q] * double[c][q]
         return carry
 
     lax.fori_loop(0, image_ref.shape[0] // block, step, 0)
@@ -193,30 +210,29 @@
     head_ref[0:1, classes : classes + labels] = lab_ref[...]
 
 
-def own_body(side, pixels, block, own_ref, sup_ref, sum_ref, plane_ref, state_ref):
+def own_body(side, block, own_ref, sup_ref, sum_ref, plane_ref, state_ref):
     grid = Grid(side)
     support = [
         grid.swap([sup_ref[c * SUB : (c + 1) * SUB, :]] * grid.fold) for c in range(CH)
     ]
-    levels, gains = self_levels(grid, support)
-    gains2, decay, slope_of = [], [], []
-    for level, gain in zip(levels, gains):
-        gains2.append([2.0 * g for g in gain])
-        decay.append([-(g * g) for g in gain])
-        slope_of.append(
-            [(2.0 * LATER) * (g * g) * lax.rsqrt(1.0 + 4.0 * x) for x, g in zip(level, gain)]
-        )
-    state = (support, gains2, decay, slope_of)
+    gains = self_gains(grid, support)
+    state = (
+        [[FIRST * x for x in rows] for rows in support],
+        [[2.0 * x for x in rows] for rows in support],
+        [[2.0 * g for g in gain] for gain in gains],
+        [[-(g * g) for g in gain] for gain in gains],
+        [[2.0 * (g * g * g) * lax.rsqrt(2.0 - g * g) for g in gain] for gain in gains],
+    )
     for part, arrays in enumerate(state):
-        for layer in range(DEPTH):
+        for k in range(DEPTH):
             for q in range(grid.fold):
-                state_ref[part, layer, q] = arrays[layer][q]
+                state_ref[part, k, q] = arrays[k][q]
 
     def sum_of(k, rows):
         for g in range(rows.shape[0]):
             sum_ref[pl.ds(k * rows.shape[0] + g, 1)] = rows[g : g + 1]
 
-    pairs_of(grid, pixels, block, own_ref, state, plane_ref, sum_of)
+    pairs_of(grid, block, own_ref, state, plane_ref, sum_of)
 
 
 def other_body(
@@ -231,7 +247,7 @@
         sums[pl.ds(core * groups + g, 1)] = own_sum_ref[g : g + 1]
     state = [
         [[state_ref[part, layer, q] for q in range(grid.fold)] for layer in range(DEPTH)]
-        for part in range(4)
+        for part in range(PARTS)
     ]
 
     def sum_of(k, rows):
@@ -239,7 +255,7 @@
         for g in range(rows.shape[0]):
             sums[pl.ds(base + g, 1)] = rows[g : g + 1]
 
-    pairs_of(grid, pixels, block, oth_ref, state, plane_ref, sum_of)
+    pairs_of(grid, block, oth_ref, state, plane_ref, sum_of)
 
     count = 2 * half
     lane = lax.broadcasted_iota(jnp.int32, (LANE, count), 0)
@@ -263,8 +279,8 @@
 
 
 def final_body(
-    side, row_of, index_of, all_ref, plane0_ref, plane1_ref, grad_ref, res_ref,
-    weight, group_weight, misfits,
+    side, pixels, row_of, index_of, all_ref, plane0_ref, plane1_ref, grad_ref, res_ref,
+    group_weight,
 ):
     grid = Grid(side)
     fold = grid.fold
@@ -276,26 +292,24 @@
     theta = all_ref[:, 0, 0:count]
     coeffs = all_ref[:, 0, width : width + classes]
     labels = all_ref[:, 0, width + classes : width + 2 * classes]
-    misfit = (
-        lax.dot_general(
-            theta,
-            coeffs,
-            (((0,), (0,)), ((), ())),
-            precision=lax.Precision.HIGHEST,
-            preferred_element_type=jnp.float32,
-        )
-        - labels
-    )
     own_coeffs = all_ref[me, :, width : width + classes]
-    cot = jnp.sum(misfit * own_coeffs, axis=1, keepdims=True)
-    weight[...] = jnp.broadcast_to(cot, weight.shape)
-    place = lax.broadcasted_iota(jnp.int32, group_weight.shape, 1) // side
-    rows = weight[pl.ds(0, 2 * groups, stride=fold), :]
-    for i in range(1, fold):
-        rows = jnp.where(place == i, weight[pl.ds(i, 2 * groups, stride=fold), :], rows)
-    group_weight[...] = rows
-    misfits[...] = misfit
-    res_ref[...] = misfits[pl.ds(me, 1), 0 : res_ref.shape[-1]]
+    gram = jnp.sum(coeffs * own_coeffs, axis=1, keepdims=True)
+    known = jnp.sum(labels * own_coeffs, axis=1, keepdims=True)
+    source = lax.broadcasted_iota(jnp.int32, theta.shape, 0)
+    image = lax.broadcasted_iota(jnp.int32, theta.shape, 1)
+    terms = theta * gram - jnp.where(source == image, known, 0.0)
+    cot = jnp.broadcast_to(jnp.sum(terms, axis=0, keepdims=True), (SUB, count))
+    if count % LANE:
+        cot = jnp.concatenate([cot, jnp.zeros((SUB, LANE - count % LANE), jnp.float32)], axis=1)
+    for g in range(2 * groups):
+        tile, lane = divmod(g * fold, LANE)
+        part = cot[:, tile * LANE : (tile + 1) * LANE]
+        group_weight[g : g + 1] = jnp.take_along_axis(part, grid.place + lane, axis=1)[0:1]
+
+    share = jnp.sum(jnp.where(image == me, theta, 0.0), axis=1, keepdims=True)
+    predicted = jnp.sum(share * coeffs, axis=0, keepdims=True)
+    own_labels = all_ref[me, :, width + classes : width + 2 * classes]
+    res_ref[...] = (predicted - own_labels)[:, 0 : res_ref.shape[-1]]
 
     block = math.gcd(groups, 4)
 
@@ -311,6 +325,7 @@
         acc = step(plane0_ref, core * groups, k, acc)
         return tuple(step(plane1_ref, (1 - core) * groups, k, acc))
 
+    factor = (WEIGHT_VAR * TWO_PI / pixels) * LATER ** (DEPTH - 1) * FIRST
     zero = jnp.zeros((SUB, LANE), jnp.float32)
     acc = lax.fori_loop(0, groups // block, both, (zero,) * (CH * fold))
     for c in range(CH):
@@ -321,7 +336,7 @@
                 x = x + pltpu.roll(x, shift, 1)
                 shift //= 2
             out = x if out is None else jnp.where(grid.place == q, x, out)
-        grad_ref[c * SUB : (c + 1) * SUB, :] = out
+        grad_ref[c * SUB : (c + 1) * SUB, :] = factor * out
 
 
 def local(support, coeffs, targets, labels):
@@ -371,11 +386,11 @@
 
     planes = jax.ShapeDtypeStruct((groups, CH, fold, SUB, LANE), f32)
     sums, planes0, state = pl.pallas_call(
-        functools.partial(own_body, side, pixels, block),
+        functools.partial(own_body, side, block),
         out_shape=(
             jax.ShapeDtypeStruct((groups, LANE), f32),
             planes,
-            jax.ShapeDtypeStruct((4, DEPTH, fold, SUB, LANE), f32),
+            jax.ShapeDtypeStruct((PARTS, DEPTH, fold, SUB, LANE), f32),
         ),
         in_specs=[vmem] * 2,
         out_specs=[vmem] * 3,
@@ -403,18 +418,14 @@
         return (core * lax.axis_size("tgt") + tgt) * lax.axis_size("row") + place
 
     grad, residual = pl.pallas_call(
-        functools.partial(final_body, side, row_of, index_of),
+        functools.partial(final_body, side, pixels, row_of, index_of),
         out_shape=(
             jax.ShapeDtypeStruct(sup.shape, f32),
             jax.ShapeDtypeStruct(labels.shape, f32),
         ),
         in_specs=[vmem] * 3,
         out_specs=[vmem] * 2,
-        scratch_shapes=[
-            pltpu.VMEM((count, LANE), f32),
-            pltpu.VMEM((2 * groups, LANE), f32),
-            pltpu.VMEM((count, classes), f32),
-        ],
+        scratch_shapes=[pltpu.VMEM((2 * groups, LANE), f32)],
         compiler_params=limit,
         name="final",
     )(rows, planes0, planes1)

time: 31.7 us -> 31.5 us (level)
  transfers between devices with their start and end apart: 1 -> 1, of which waited for: 1 -> 1; matrix products, arithmetic and copies ran while one was open for 0% -> 0% of each run, Pallas kernels for 4% -> 3%
where the time goes in v4:
time: 31.5 us; the launch traced here: 31.3 us
  blocking collectives  26.3 us (83%)
  Pallas kernels  3.91 us (12%)
  between operations  0.66 us (2%)
  waiting for transfers between devices  0.36 us (1%)
    all_to_all x1, blocking collectives, local(): own = lax.all_to_all(images, ('tgt', 'row'), 0, 0, tiled=True)  17.3 us
    all_to_all x1, blocking collectives, local(): lax.all_to_all(jnp.broadcast_to(row[None], (count, 1, width)), ('core', '...  8.96 us
    pallas_call x1, Pallas kernels, local(): pl.pallas_call(functools.partial(other_body, side, pixels, block, row_of[...  1.08 us
    pallas_call x1, Pallas kernels, local(): pl.pallas_call(functools.partial(own_body, side, block), out_shape=(jax.S...  1.07 us
    pallas_call x1, Pallas kernels, local(): pl.pallas_call(functools.partial(final_body, side, pixels, row_of, index_...  1 us
    pallas_call x1, Pallas kernels, local(): pl.pallas_call(functools.partial(first_body, classes), out_shape=(jax.Sha...  0.77 us
  transfers between devices with their start and end apart: 1, of which 1 were waited for; matrix products, arithmetic and copies ran while one was open for 0% of the time, Pallas kernels for 3%

profile of v4, /device:TPU:0, one launch (start us, length us, event | category | flops | bytes accessed | tf_op | source)
XLA Modules:
  0.0 31.3 jit_solution(11944372833889721408)
XLA Ops:
  0.6 0.8 %first.1 = (f32[16,24,128]{2,1,0:T(8,128)S(1)}, f32[24,128]{1,0:T(8,128)S(1)}, f32[1,256]{1,0:T(1,128)S(1)}) custom-call(f32[24,128]{1,0:T(8,128)} %bitcast.3, f32[24,128]{1,0:T(8,128)} %bitcast.4, f32[4,100]{1,0:T(4,128)} %coef_hbm.1, f32[1,100]{1,0:T(1,128)} %lab_hbm.1), custom_call_target="tpu_custom_call" | custom-call | tf_op jit(solution)/shard_map/first/pallas_call | solution.py:366
  1.4 17.3 %all_to_all.10.own_ref = f32[16,24,128]{2,1,0:T(8,128)S(1)} all-to-all(f32[16,24,128]{2,1,0:T(8,128)S(1)} %get-tuple-element.12), channel_id=1, replica_groups=mesh['tgt'=4,'row'=4,'core'=2] {'tgt','row'}, dimensions={0} | all-to-all | bytes 393216 | tf_op jit(solution)/shard_map/all_to_all | solution.py:384
  18.7 0.0 collective-permute-start
  18.7 1.1 %own.1 = (f32[4,128]{1,0:T(4,128)S(1)}, f32[4,3,4,8,128]{4,3,2,1,0:T(8,128)S(1)}, f32[5,3,4,8,128]{4,3,2,1,0:T(8,128)S(1)}) custom-call(f32[16,24,128]{2,1,0:T(8,128)S(1)} %all_to_all.10.own_ref, f32[24,128]{1,0:T(8,128)S(1)} %get-tuple-element.13.sup_ref), custom_call_target="tpu_custom_call" | custom-call | flops 4915200 | bytes 393216 | tf_op jit(solution)/shard_map/own/pallas_call | solution.py:388
  19.8 0.4 %collective-permute-done.oth_ref = f32[16,24,128]{2,1,0:T(8,128)S(1)} collective-permute-done((f32[16,24,128]{2,1,0:T(8,128)S(1)}, f32[16,24,128]{2,1,0:T(8,128)S(1)}, u32[]{:S(2)}, u32[]{:S(2)}) %collective-permute-start) | collective-permute-done | bytes 196640 | tf_op jit(solution)/shard_map/ppermute | solution.py:385
  20.2 1.1 %other.1 = (f32[1,384]{1,0:T(1,128)S(1)}, f32[4,3,4,8,128]{4,3,2,1,0:T(8,128)S(1)}) custom-call(f32[16,24,128]{2,1,0:T(8,128)S(1)} %collective-permute-done.oth_ref, f32[5,3,4,8,128]{4,3,2,1,0:T(8,128)S(1)} %get-tuple-element.14.state_ref, f32[4,128]{1,0:T(4,128)S(1)} %get-tuple-element.15.own_sum_ref, f32[1,256]{1,0:T(1,128)S(1)} %get-tuple-element.16.head_ref), custom_call_target="tpu_custom_call" | custom-call | flops 4915200 | bytes 393216 | tf_op jit(solution)/shard_map/other/pallas_call | solution.py:401
  21.3 9.0 %all_to_all.11.all_ref = f32[32,1,384]{2,1,0:T(1,128)S(1)} all-to-all(f32[32,1,384]{2,1,0:T(1,128)S(1)} %broadcast_in_dim.9), channel_id=1, replica_groups=mesh['tgt'=4,'row'=4,'core'=2] {'core','tgt','row'}, dimensions={0} | all-to-all | bytes 98304 | tf_op jit(solution)/shard_map/all_to_all | solution.py:412
  30.3 1.0 %final.1 = (f32[24,128]{1,0:T(8,128)}, f32[1,100]{1,0:T(1,128)}) custom-call(f32[32,1,384]{2,1,0:T(1,128)S(1)} %all_to_all.11.all_ref, f32[4,3,4,8,128]{4,3,2,1,0:T(8,128)S(1)} %get-tuple-element.18.plane0_ref, f32[4,3,4,8,128]{4,3,2,1,0:T(8,128)S(1)} %get-tuple-element.19.plane1_ref), custom_call_target="tpu_custom_call" | custom-call | tf_op jit(solution)/shard_map/final/pallas_call | solution.py:420
  (2 shorter events, 0.1 us)
Async XLA Ops:
  18.7 1.4 %collective-permute-start = (f32[16,24,128]{2,1,0:T(8,128)S(1)}, f32[16,24,128]{2,1,0:T(8,128)S(1)}, u32[]{:S(2)}, u32[]{:S(2)}) collective-permute-start(f32[16,24,128]{2,1,0:T(8,128)S(1)} %all_to_all.10.own_ref), channel_id=1, source_target_pairs={{0,1},{1,0},{2,3},{3,2},{4,5},{5,4},{6,7},{7,6},{8,9},{9,8},{10,11... | collective-permute-start | bytes 589832 | tf_op jit(solution)/shard_map/ppermute | solution.py:385

commit v5 on v4

--- a/solution.py
+++ b/solution.py
@@ -16,7 +16,7 @@
 SUB = 8
 LANE = 128
 TWO_PI = 2.0 / math.pi
-PARTS = 5
+PARTS = 4
 FIRST = WEIGHT_VAR / (9 * CH)
 LATER = WEIGHT_VAR * TWO_PI / 9
 
@@ -121,8 +121,7 @@
         return out
 
 
-def self_gains(grid, image):
-    energy = [sum(x * x for x in rows) for rows in zip(*image)]
+def self_gains(grid, energy):
     start = 1.0 + 2.0 * BIAS_VAR
     gain = [lax.rsqrt((2.0 * FIRST) * x + start) for x in grid.box(energy)]
     gains = [gain]
@@ -142,17 +141,16 @@
     def step(k, carry):
         at = pl.ds(k * block, block)
         to = pl.ds(k * (block // fold), block // fold)
-        target = []
-        for c in range(CH):
+
+        def channel(c):
             x = image_ref[at, c * SUB : (c + 1) * SUB, :].reshape(block // fold, fold, SUB, LANE)
-            target.append(grid.swap([x[:, i] for i in range(fold)]))
-        tgt_gains = self_gains(grid, target)
-        spread = grid.box(
-            [
-                sum(s * t for s, t in zip(row_s, row_t))
-                for row_s, row_t in zip(zip(*scaled), zip(*target))
-            ]
-        )
+            return [x[:, i] for i in range(fold)]
+
+        target = [channel(c) for c in range(CH)]
+        energy = [sum(x * x for x in images) for images in zip(*target)]
+        product = [sum(s * x for s, x in zip(scaled, images)) for images in zip(*target)]
+        tgt_gains = self_gains(grid, grid.swap(energy))
+        spread = grid.box(grid.swap(product))
         gains, corrs, rests = [], [], []
         for layer in range(DEPTH):
             gain = [s * t for s, t in zip(gains2[layer], tgt_gains[layer])]
@@ -183,8 +181,8 @@
         grad = grid.box([s * g for s, g in zip(slope, gains[0])])
         energy = grid.box(carried)
         for c in range(CH):
-            for q in range(fold):
-                plane_ref[to, c, q] = grad[q] * target[c][q] + energy[q] * double[c][q]
+            for q, x in enumerate(grid.swap(channel(c))):
+                plane_ref[to, c, q] = grad[q] * x + energy[q] * double[c][q]
         return carry
 
     lax.fori_loop(0, image_ref.shape[0] // block, step, 0)
@@ -212,12 +210,10 @@
 
 def own_body(side, block, own_ref, sup_ref, sum_ref, plane_ref, state_ref):
     grid = Grid(side)
-    support = [
-        grid.swap([sup_ref[c * SUB : (c + 1) * SUB, :]] * grid.fold) for c in range(CH)
-    ]
-    gains = self_gains(grid, support)
+    image = [sup_ref[c * SUB : (c + 1) * SUB, :] for c in range(CH)]
+    support = [grid.swap([x] * grid.fold) for x in image]
+    gains = self_gains(grid, [sum(x * x for x in rows) for rows in zip(*support)])
     state = (
-        [[FIRST * x for x in rows] for rows in support],
         [[2.0 * x for x in rows] for rows in support],
         [[2.0 * g for g in gain] for gain in gains],
         [[-(g * g) for g in gain] for gain in gains],
@@ -227,6 +223,7 @@
         for k in range(DEPTH):
             for q in range(grid.fold):
                 state_ref[part, k, q] = arrays[k][q]
+    state = ([FIRST * x for x in image],) + state
 
     def sum_of(k, rows):
         for g in range(rows.shape[0]):
@@ -236,7 +233,7 @@
 
 
 def other_body(
-    side, pixels, block, width, oth_ref, state_ref, own_sum_ref, head_ref,
+    side, pixels, block, width, oth_ref, sup_ref, state_ref, own_sum_ref, head_ref,
     row_ref, plane_ref, sums,
 ):
     grid = Grid(side)
@@ -245,7 +242,7 @@
     core = lax.axis_index("core")
     for g in range(groups):
         sums[pl.ds(core * groups + g, 1)] = own_sum_ref[g : g + 1]
-    state = [
+    state = [[FIRST * sup_ref[c * SUB : (c + 1) * SUB, :] for c in range(CH)]] + [
         [[state_ref[part, layer, q] for q in range(grid.fold)] for layer in range(DEPTH)]
         for part in range(PARTS)
     ]
@@ -273,9 +270,13 @@
     total = jnp.sum(
         jnp.where(image // grid.fold == group, total, 0.0), axis=0, keepdims=True
     )
-    row_ref[:, 0:width] = jnp.zeros((1, width), jnp.float32)
-    row_ref[:, 0:count] = (WEIGHT_VAR * TWO_PI / pixels) * total + BIAS_VAR
-    row_ref[:, width:] = head_ref[...]
+    theta = (WEIGHT_VAR * TWO_PI / pixels) * total + BIAS_VAR
+    if width > count:
+        theta = jnp.concatenate([theta, jnp.zeros((1, width - count), jnp.float32)], axis=1)
+    head = head_ref[...]
+    for k in range(count):
+        row_ref[k, :, 0:width] = theta
+        row_ref[k, :, width:] = head
 
 
 def final_body(
@@ -398,19 +399,19 @@
         cost_estimate=effort,
         name="own",
     )(own, sup)
-    row, planes1 = pl.pallas_call(
+    rows, planes1 = pl.pallas_call(
         functools.partial(other_body, side, pixels, block, row_of["theta"]),
-        out_shape=(jax.ShapeDtypeStruct((1, width), f32), planes),
-        in_specs=[vmem] * 4,
+        out_shape=(jax.ShapeDtypeStruct((count, 1, width), f32), planes),
+        in_specs=[vmem] * 5,
         out_specs=[vmem] * 2,
         scratch_shapes=[pltpu.VMEM((2 * groups, LANE), f32)],
         compiler_params=limit,
         cost_estimate=effort,
         name="other",
-    )(oth, state, sums, head)
+    )(oth, sup, state, sums, head)
 
     rows = lax.all_to_all(
-        jnp.broadcast_to(row[None], (count, 1, width)), ("core", "tgt", "row"), 0, 0, tiled=True
+        rows, ("core", "tgt", "row"), 0, 0, tiled=True
     )
 
     def index_of():

time: 31.5 us -> 31.4 us (level)
  no operation moved by 1% of the time
where the time goes in v5:
time: 31.4 us; the launch traced here: 31.1 us
  blocking collectives  26.3 us (84%)
  Pallas kernels  3.76 us (12%)
  between operations  0.66 us (2%)
  waiting for transfers between devices  0.43 us (1%)
    all_to_all x1, blocking collectives, local(): own = lax.all_to_all(images, ('tgt', 'row'), 0, 0, tiled=True)  17.3 us
    all_to_all x1, blocking collectives, local(): rows = lax.all_to_all(rows, ('core', 'tgt', 'row'), 0, 0, tiled=True)  8.96 us
    pallas_call x1, Pallas kernels, local(): pl.pallas_call(functools.partial(own_body, side, block), out_shape=(jax.S...  1.01 us
    pallas_call x1, Pallas kernels, local(): pl.pallas_call(functools.partial(final_body, side, pixels, row_of, index_...  1 us
    pallas_call x1, Pallas kernels, local(): pl.pallas_call(functools.partial(other_body, side, pixels, block, row_of[...  0.98 us
    pallas_call x1, Pallas kernels, local(): pl.pallas_call(functools.partial(first_body, classes), out_shape=(jax.Sha...  0.77 us
  transfers between devices with their start and end apart: 1, of which 1 were waited for; matrix products, arithmetic and copies ran while one was open for 0% of the time, Pallas kernels for 3%

profile of v5, /device:TPU:0, one launch (start us, length us, event | category | flops | bytes accessed | tf_op | source)
XLA Modules:
  0.0 31.1 jit_solution(11516690253264245689)
XLA Ops:
  0.6 0.8 %first.1 = (f32[16,24,128]{2,1,0:T(8,128)S(1)}, f32[24,128]{1,0:T(8,128)S(1)}, f32[1,256]{1,0:T(1,128)S(1)}) custom-call(f32[24,128]{1,0:T(8,128)} %bitcast.3, f32[24,128]{1,0:T(8,128)} %bitcast.4, f32[4,100]{1,0:T(4,128)} %coef_hbm.1, f32[1,100]{1,0:T(1,128)} %lab_hbm.1), custom_call_target="tpu_custom_call" | custom-call | tf_op jit(solution)/shard_map/first/pallas_call | solution.py:367
  1.4 17.3 %all_to_all.10.own_ref = f32[16,24,128]{2,1,0:T(8,128)S(1)} all-to-all(f32[16,24,128]{2,1,0:T(8,128)S(1)} %get-tuple-element.12), channel_id=1, replica_groups=mesh['tgt'=4,'row'=4,'core'=2] {'tgt','row'}, dimensions={0} | all-to-all | bytes 393216 | tf_op jit(solution)/shard_map/all_to_all | solution.py:385
  18.7 0.0 collective-permute-start
  18.7 1.0 %own.1 = (f32[4,128]{1,0:T(4,128)S(1)}, f32[4,3,4,8,128]{4,3,2,1,0:T(8,128)S(1)}, f32[4,3,4,8,128]{4,3,2,1,0:T(8,128)S(1)}) custom-call(f32[16,24,128]{2,1,0:T(8,128)S(1)} %all_to_all.10.own_ref, f32[24,128]{1,0:T(8,128)S(1)} %get-tuple-element.13.sup_ref), custom_call_target="tpu_custom_call" | custom-call | flops 4915200 | bytes 393216 | tf_op jit(solution)/shard_map/own/pallas_call | solution.py:389
  19.7 0.4 %collective-permute-done.oth_ref = f32[16,24,128]{2,1,0:T(8,128)S(1)} collective-permute-done((f32[16,24,128]{2,1,0:T(8,128)S(1)}, f32[16,24,128]{2,1,0:T(8,128)S(1)}, u32[]{:S(2)}, u32[]{:S(2)}) %collective-permute-start) | collective-permute-done | bytes 196640 | tf_op jit(solution)/shard_map/ppermute | solution.py:386
  20.2 1.0 %other.1 = (f32[32,1,384]{2,1,0:T(1,128)S(1)}, f32[4,3,4,8,128]{4,3,2,1,0:T(8,128)S(1)}) custom-call(f32[16,24,128]{2,1,0:T(8,128)S(1)} %collective-permute-done.oth_ref, f32[24,128]{1,0:T(8,128)S(1)} %get-tuple-element.13.sup_ref, f32[4,3,4,8,128]{4,3,2,1,0:T(8,128)S(1)} %get-tuple-element.14.state_ref, f32[4,128]{1,0:T(4,128)S(1)} %get-tuple-element.15.own_sum_ref, ...), custom_call_target="tpu_custom_call" | custom-call | flops 4915200 | bytes 393216 | tf_op jit(solution)/shard_map/other/pallas_call | solution.py:402
  21.1 9.0 %all_to_all.11.all_ref = f32[32,1,384]{2,1,0:T(1,128)S(1)} all-to-all(f32[32,1,384]{2,1,0:T(1,128)S(1)} %get-tuple-element.17), channel_id=1, replica_groups=mesh['tgt'=4,'row'=4,'core'=2] {'core','tgt','row'}, dimensions={0} | all-to-all | bytes 98304 | tf_op jit(solution)/shard_map/all_to_all | solution.py:413
  30.1 1.0 %final.1 = (f32[24,128]{1,0:T(8,128)}, f32[1,100]{1,0:T(1,128)}) custom-call(f32[32,1,384]{2,1,0:T(1,128)S(1)} %all_to_all.11.all_ref, f32[4,3,4,8,128]{4,3,2,1,0:T(8,128)S(1)} %get-tuple-element.18.plane0_ref, f32[4,3,4,8,128]{4,3,2,1,0:T(8,128)S(1)} %get-tuple-element.19.plane1_ref), custom_call_target="tpu_custom_call" | custom-call | tf_op jit(solution)/shard_map/final/pallas_call | solution.py:421
Async XLA Ops:
  18.7 1.4 %collective-permute-start = (f32[16,24,128]{2,1,0:T(8,128)S(1)}, f32[16,24,128]{2,1,0:T(8,128)S(1)}, u32[]{:S(2)}, u32[]{:S(2)}) collective-permute-start(f32[16,24,128]{2,1,0:T(8,128)S(1)} %all_to_all.10.own_ref), channel_id=1, source_target_pairs={{0,1},{1,0},{2,3},{3,2},{4,5},{5,4},{6,7},{7,6},{8,9},{9,8},{10,11... | collective-permute-start | bytes 589832 | tf_op jit(solution)/shard_map/ppermute | solution.py:386

commit v6 on v5

--- a/solution.py
+++ b/solution.py
@@ -65,6 +65,10 @@
 def arcsine_inner(x, scale):
     z = x * x
     return x * horner(z, WIDE, scale), 1.0 - z
+
+
+def chip_order(tgts, rows):
+    return [(t, (k + 1) % rows) for t in reversed(range(tgts)) for k in range(rows)]
 
 
 class Grid:
@@ -382,7 +386,11 @@
         compiler_params=limit,
         name="first",
     )(*(pltpu.with_memory_space_constraint(x, pltpu.HBM) for x in inputs))
-    own = lax.all_to_all(images, ("tgt", "row"), 0, 0, tiled=True)
+    axes = ("tgt", "row", "core")
+    tgts, rows = lax.axis_size("tgt"), lax.axis_size("row")
+    order = chip_order(tgts, rows)
+    halves = [[(t * rows + r) * 2 + core for t, r in order] for core in range(2)]
+    own = lax.all_to_all(images, axes, 0, 0, axis_index_groups=halves, tiled=True)
     oth = lax.ppermute(own, "core", [(0, 1), (1, 0)])
 
     planes = jax.ShapeDtypeStruct((groups, CH, fold, SUB, LANE), f32)
@@ -399,7 +407,7 @@
         cost_estimate=effort,
         name="own",
     )(own, sup)
-    rows, planes1 = pl.pallas_call(
+    theta_rows, planes1 = pl.pallas_call(
         functools.partial(other_body, side, pixels, block, row_of["theta"]),
         out_shape=(jax.ShapeDtypeStruct((count, 1, width), f32), planes),
         in_specs=[vmem] * 5,
@@ -410,13 +418,13 @@
         name="other",
     )(oth, sup, state, sums, head)
 
-    rows = lax.all_to_all(
-        rows, ("core", "tgt", "row"), 0, 0, tiled=True
+    theta_rows = lax.all_to_all(
+        theta_rows, axes, 0, 0, axis_index_groups=[halves[0] + halves[1]], tiled=True
     )
 
     def index_of():
-        tgt, place, core = (lax.axis_index(a) for a in ("tgt", "row", "core"))
-        return (core * lax.axis_size("tgt") + tgt) * lax.axis_size("row") + place
+        t, r, core = (lax.axis_index(a) for a in axes)
+        return core * chips + (tgts - 1 - t) * rows + lax.rem(r + rows - 1, rows)
 
     grad, residual = pl.pallas_call(
         functools.partial(final_body, side, pixels, row_of, index_of),
@@ -429,7 +437,7 @@
         scratch_shapes=[pltpu.VMEM((2 * groups, LANE), f32)],
         compiler_params=limit,
         name="final",
-    )(rows, planes0, planes1)
+    )(theta_rows, planes0, planes1)
     return grad.reshape(support.shape), residual
 
 

time: 31.4 us -> 29.6 us (0.943)
  blocking collectives: 26.3 us -> 24.4 us
    all_to_all x2, blocking collectives: 26.3 us -> 24.4 us  [the longest x1 14.6 us: local(): lax.all_to_all(images, axes, 0, 0, axis_index_groups=halves, tiled=True)]
where the time goes in v6:
time: 29.6 us; the launch traced here: 29.3 us
  blocking collectives  24.4 us (82%)
  Pallas kernels  3.75 us (13%)
  between operations  0.66 us (2%)
  waiting for transfers between devices  0.43 us (1%)
    all_to_all x1, blocking collectives, local(): lax.all_to_all(images, axes, 0, 0, axis_index_groups=halves, tiled=True)  14.6 us
    all_to_all x1, blocking collectives, local(): lax.all_to_all(theta_rows, axes, 0, 0, axis_index_groups=[halves[0] + hal...  9.83 us
    pallas_call x1, Pallas kernels, local(): pl.pallas_call(functools.partial(own_body, side, block), out_shape=(jax.S...  1.01 us
    pallas_call x1, Pallas kernels, local(): pl.pallas_call(functools.partial(final_body, side, pixels, row_of, index_...  1 us
    pallas_call x1, Pallas kernels, local(): pl.pallas_call(functools.partial(other_body, side, pixels, block, row_of[...  0.98 us
    pallas_call x1, Pallas kernels, local(): pl.pallas_call(functools.partial(first_body, classes), out_shape=(jax.Sha...  0.77 us
  transfers between devices with their start and end apart: 1, of which 1 were waited for; matrix products, arithmetic and copies ran while one was open for 0% of the time, Pallas kernels for 3%

profile of v6, /device:TPU:0, one launch (start us, length us, event | category | flops | bytes accessed | tf_op | source)
XLA Modules:
  0.0 29.3 jit_solution(467171313393451940)
XLA Ops:
  0.6 0.8 %first.1 = (f32[16,24,128]{2,1,0:T(8,128)S(1)}, f32[24,128]{1,0:T(8,128)S(1)}, f32[1,256]{1,0:T(1,128)S(1)}) custom-call(f32[24,128]{1,0:T(8,128)} %bitcast.3, f32[24,128]{1,0:T(8,128)} %bitcast.4, f32[4,100]{1,0:T(4,128)} %coef_hbm.1, f32[1,100]{1,0:T(1,128)} %lab_hbm.1), custom_call_target="tpu_custom_call" | custom-call | tf_op jit(solution)/shard_map/first/pallas_call | solution.py:371
  1.4 14.6 %all_to_all.10.own_ref = f32[16,24,128]{2,1,0:T(8,128)S(1)} all-to-all(f32[16,24,128]{2,1,0:T(8,128)S(1)} %get-tuple-element.12), channel_id=1, replica_groups={{26,28,30,24,18,20,22,16,10,12,14,8,2,4,6,0},{27,29,31,25,19,21,23,17,1..., dimensions={0} | all-to-all | bytes 393216 | tf_op jit(solution)/shard_map/all_to_all | solution.py:393
  16.0 0.0 collective-permute-start
  16.0 1.0 %own.1 = (f32[4,128]{1,0:T(4,128)S(1)}, f32[4,3,4,8,128]{4,3,2,1,0:T(8,128)S(1)}, f32[4,3,4,8,128]{4,3,2,1,0:T(8,128)S(1)}) custom-call(f32[16,24,128]{2,1,0:T(8,128)S(1)} %all_to_all.10.own_ref, f32[24,128]{1,0:T(8,128)S(1)} %get-tuple-element.13.sup_ref), custom_call_target="tpu_custom_call" | custom-call | flops 4915200 | bytes 393216 | tf_op jit(solution)/shard_map/own/pallas_call | solution.py:397
  17.0 0.4 %collective-permute-done.oth_ref = f32[16,24,128]{2,1,0:T(8,128)S(1)} collective-permute-done((f32[16,24,128]{2,1,0:T(8,128)S(1)}, f32[16,24,128]{2,1,0:T(8,128)S(1)}, u32[]{:S(2)}, u32[]{:S(2)}) %collective-permute-start) | collective-permute-done | bytes 196640 | tf_op jit(solution)/shard_map/ppermute | solution.py:394
  17.5 1.0 %other.1 = (f32[32,1,384]{2,1,0:T(1,128)S(1)}, f32[4,3,4,8,128]{4,3,2,1,0:T(8,128)S(1)}) custom-call(f32[16,24,128]{2,1,0:T(8,128)S(1)} %collective-permute-done.oth_ref, f32[24,128]{1,0:T(8,128)S(1)} %get-tuple-element.13.sup_ref, f32[4,3,4,8,128]{4,3,2,1,0:T(8,128)S(1)} %get-tuple-element.14.state_ref, f32[4,128]{1,0:T(4,128)S(1)} %get-tuple-element.15.own_sum_ref, ...), custom_call_target="tpu_custom_call" | custom-call | flops 4915200 | bytes 393216 | tf_op jit(solution)/shard_map/other/pallas_call | solution.py:410
  18.5 9.8 %all_to_all.11.all_ref = f32[32,1,384]{2,1,0:T(1,128)S(1)} all-to-all(f32[32,1,384]{2,1,0:T(1,128)S(1)} %get-tuple-element.17), channel_id=1, replica_groups={{26,28,30,24,18,20,22,16,10,12,14,8,2,4,6,0,27,29,31,25,19,21,23,17,11,..., dimensions={0} | all-to-all | bytes 98304 | tf_op jit(solution)/shard_map/all_to_all | solution.py:421
  28.3 1.0 %final.1 = (f32[24,128]{1,0:T(8,128)}, f32[1,100]{1,0:T(1,128)}) custom-call(f32[32,1,384]{2,1,0:T(1,128)S(1)} %all_to_all.11.all_ref, f32[4,3,4,8,128]{4,3,2,1,0:T(8,128)S(1)} %get-tuple-element.18.plane0_ref, f32[4,3,4,8,128]{4,3,2,1,0:T(8,128)S(1)} %get-tuple-element.19.plane1_ref), custom_call_target="tpu_custom_call" | custom-call | tf_op jit(solution)/shard_map/final/pallas_call | solution.py:429
Async XLA Ops:
  16.0 1.4 %collective-permute-start = (f32[16,24,128]{2,1,0:T(8,128)S(1)}, f32[16,24,128]{2,1,0:T(8,128)S(1)}, u32[]{:S(2)}, u32[]{:S(2)}) collective-permute-start(f32[16,24,128]{2,1,0:T(8,128)S(1)} %all_to_all.10.own_ref), channel_id=1, source_target_pairs={{0,1},{1,0},{2,3},{3,2},{4,5},{5,4},{6,7},{7,6},{8,9},{9,8},{10,11... | collective-permute-start | bytes 589832 | tf_op jit(solution)/shard_map/ppermute | solution.py:394

commit v7 on v6

--- a/solution.py
+++ b/solution.py
@@ -68,7 +68,7 @@
 
 
 def chip_order(tgts, rows):
-    return [(t, (k + 1) % rows) for t in reversed(range(tgts)) for k in range(rows)]
+    return [(t, (1 + rows - k) % rows) for t in reversed(range(tgts)) for k in range(rows)]
 
 
 class Grid:
@@ -424,7 +424,7 @@
 
     def index_of():
         t, r, core = (lax.axis_index(a) for a in axes)
-        return core * chips + (tgts - 1 - t) * rows + lax.rem(r + rows - 1, rows)
+        return core * chips + (tgts - 1 - t) * rows + lax.rem(1 + rows - r, rows)
 
     grad, residual = pl.pallas_call(
         functools.partial(final_body, side, pixels, row_of, index_of),

time: 29.6 us -> 29.4 us (level)
  no operation moved by 1% of the time
where the time goes in v7:
time: 29.4 us; the launch traced here: 29.1 us
  blocking collectives  24.3 us (83%)
  Pallas kernels  3.75 us (13%)
  between operations  0.66 us (2%)
  waiting for transfers between devices  0.43 us (1%)
    all_to_all x1, blocking collectives, local(): lax.all_to_all(images, axes, 0, 0, axis_index_groups=halves, tiled=True)  14.6 us
    all_to_all x1, blocking collectives, local(): lax.all_to_all(theta_rows, axes, 0, 0, axis_index_groups=[halves[0] + hal...  9.67 us
    pallas_call x1, Pallas kernels, local(): pl.pallas_call(functools.partial(own_body, side, block), out_shape=(jax.S...  1.01 us
    pallas_call x1, Pallas kernels, local(): pl.pallas_call(functools.partial(final_body, side, pixels, row_of, index_...  1 us
    pallas_call x1, Pallas kernels, local(): pl.pallas_call(functools.partial(other_body, side, pixels, block, row_of[...  0.98 us
    pallas_call x1, Pallas kernels, local(): pl.pallas_call(functools.partial(first_body, classes), out_shape=(jax.Sha...  0.77 us
  transfers between devices with their start and end apart: 1, of which 1 were waited for; matrix products, arithmetic and copies ran while one was open for 0% of the time, Pallas kernels for 3%

profile of v7, /device:TPU:0, one launch (start us, length us, event | category | flops | bytes accessed | tf_op | source)
XLA Modules:
  0.0 29.1 jit_solution(8158453339687312865)
XLA Ops:
  0.6 0.8 %first.1 = (f32[16,24,128]{2,1,0:T(8,128)S(1)}, f32[24,128]{1,0:T(8,128)S(1)}, f32[1,256]{1,0:T(1,128)S(1)}) custom-call(f32[24,128]{1,0:T(8,128)} %bitcast.3, f32[24,128]{1,0:T(8,128)} %bitcast.4, f32[4,100]{1,0:T(4,128)} %coef_hbm.1, f32[1,100]{1,0:T(1,128)} %lab_hbm.1), custom_call_target="tpu_custom_call" | custom-call | tf_op jit(solution)/shard_map/first/pallas_call | solution.py:371
  1.4 14.6 %all_to_all.10.own_ref = f32[16,24,128]{2,1,0:T(8,128)S(1)} all-to-all(f32[16,24,128]{2,1,0:T(8,128)S(1)} %get-tuple-element.12), channel_id=1, replica_groups={{26,24,30,28,18,16,22,20,10,8,14,12,2,0,6,4},{27,25,31,29,19,17,23,21,1..., dimensions={0} | all-to-all | bytes 393216 | tf_op jit(solution)/shard_map/all_to_all | solution.py:393
  16.0 0.0 collective-permute-start
  16.0 1.0 %own.1 = (f32[4,128]{1,0:T(4,128)S(1)}, f32[4,3,4,8,128]{4,3,2,1,0:T(8,128)S(1)}, f32[4,3,4,8,128]{4,3,2,1,0:T(8,128)S(1)}) custom-call(f32[16,24,128]{2,1,0:T(8,128)S(1)} %all_to_all.10.own_ref, f32[24,128]{1,0:T(8,128)S(1)} %get-tuple-element.13.sup_ref), custom_call_target="tpu_custom_call" | custom-call | flops 4915200 | bytes 393216 | tf_op jit(solution)/shard_map/own/pallas_call | solution.py:397
  17.0 0.4 %collective-permute-done.oth_ref = f32[16,24,128]{2,1,0:T(8,128)S(1)} collective-permute-done((f32[16,24,128]{2,1,0:T(8,128)S(1)}, f32[16,24,128]{2,1,0:T(8,128)S(1)}, u32[]{:S(2)}, u32[]{:S(2)}) %collective-permute-start) | collective-permute-done | bytes 196640 | tf_op jit(solution)/shard_map/ppermute | solution.py:394
  17.5 1.0 %other.1 = (f32[32,1,384]{2,1,0:T(1,128)S(1)}, f32[4,3,4,8,128]{4,3,2,1,0:T(8,128)S(1)}) custom-call(f32[16,24,128]{2,1,0:T(8,128)S(1)} %collective-permute-done.oth_ref, f32[24,128]{1,0:T(8,128)S(1)} %get-tuple-element.13.sup_ref, f32[4,3,4,8,128]{4,3,2,1,0:T(8,128)S(1)} %get-tuple-element.14.state_ref, f32[4,128]{1,0:T(4,128)S(1)} %get-tuple-element.15.own_sum_ref, ...), custom_call_target="tpu_custom_call" | custom-call | flops 4915200 | bytes 393216 | tf_op jit(solution)/shard_map/other/pallas_call | solution.py:410
  18.4 9.7 %all_to_all.11.all_ref = f32[32,1,384]{2,1,0:T(1,128)S(1)} all-to-all(f32[32,1,384]{2,1,0:T(1,128)S(1)} %get-tuple-element.17), channel_id=1, replica_groups={{26,24,30,28,18,16,22,20,10,8,14,12,2,0,6,4,27,25,31,29,19,17,23,21,11,..., dimensions={0} | all-to-all | bytes 98304 | tf_op jit(solution)/shard_map/all_to_all | solution.py:421
  28.1 1.0 %final.1 = (f32[24,128]{1,0:T(8,128)}, f32[1,100]{1,0:T(1,128)}) custom-call(f32[32,1,384]{2,1,0:T(1,128)S(1)} %all_to_all.11.all_ref, f32[4,3,4,8,128]{4,3,2,1,0:T(8,128)S(1)} %get-tuple-element.18.plane0_ref, f32[4,3,4,8,128]{4,3,2,1,0:T(8,128)S(1)} %get-tuple-element.19.plane1_ref), custom_call_target="tpu_custom_call" | custom-call | tf_op jit(solution)/shard_map/final/pallas_call | solution.py:429
Async XLA Ops:
  16.0 1.4 %collective-permute-start = (f32[16,24,128]{2,1,0:T(8,128)S(1)}, f32[16,24,128]{2,1,0:T(8,128)S(1)}, u32[]{:S(2)}, u32[]{:S(2)}) collective-permute-start(f32[16,24,128]{2,1,0:T(8,128)S(1)} %all_to_all.10.own_ref), channel_id=1, source_target_pairs={{0,1},{1,0},{2,3},{3,2},{4,5},{5,4},{6,7},{7,6},{8,9},{9,8},{10,11... | collective-permute-start | bytes 589832 | tf_op jit(solution)/shard_map/ppermute | solution.py:394
